TPU v7x, 32 devices: a whole 2x2x4 slice. The times are simulated.
32 devices in a mesh: vtx: 8 (over y, x, core), edg: 4 (over z).
Axes of the slice: x: 2, y: 2, z: 4, core: 2. Of those that a mesh axis runs over, the one named last changes fastest.
Arguments:
- sketch_cols: bfloat16 [131072, 128], P(('vtx', 'edg')), may hold values from -6 to 6
- edge_weight: float32 [131072], P(('vtx', 'edg')), may hold values from 0.25 to 4
- ground: float32 [16384], P('vtx'), may hold values from 0.05 to 0.5
- src_local: int32 [131072], P(('vtx', 'edg')), may hold values from 0 to 2047
- dst_index: int32 [131072], P(('vtx', 'edg')), may hold values from 0 to 2431
- send_rows: int32 [32, 8, 48], P(('vtx', 'edg')), may hold values from 0 to 2047
- edge_count: int32 [32], P(('vtx', 'edg')), may hold values from 512 to 4096, as said below
Outputs:
- solution: float32 [16384, 128], P('vtx')
- resistance: float32 [131072], P(('vtx', 'edg'))
Inputs may be any that keep to these rules, and one draw needn't show every extreme that they name: `edge_count`: edge slots of a device at positions of its count or beyond are unused. In every draw some device has all 4096 slots live.
All inputs are finite; a program needn't handle non-finite values.
Results may differ from a plain program's by a relative error of at most 0.0003.
Values sent between devices are 32-bit elements; how exact they have to be, the bound alone decides.
A program may use at most 64 MiB of HBM per device.

v0:
```python
import functools

import jax
import jax.numpy as jnp
from jax import lax
from jax.experimental import pallas as pl
from jax.experimental.pallas import tpu as pltpu
from jax.sharding import PartitionSpec as P

ITERS = 3

lam_low = 0.05
lam_high = 2.0
LANES = 128
VMEM_LIMIT = 60 * 1024 * 1024


def chebyshev_terms(steps):
    centre = (lam_high + lam_low) / 2.0
    half_width = (lam_high - lam_low) / 2.0
    sigma_val = centre / half_width
    rho_prev = 1.0 / sigma_val
    pairs = []
    for count_idx in range(steps - 1):
        rho_next = 1.0 / (2.0 * sigma_val - rho_prev)
        pairs.append((rho_next * rho_prev, 2.0 * rho_next / half_width))
        rho_prev = rho_next
    return (1.0 / centre, pairs)


def split2(x):
    hi = x.astype(jnp.bfloat16)
    lo = (x - hi.astype(jnp.float32)).astype(jnp.bfloat16)
    return hi, lo


def split3(x):
    hi = x.astype(jnp.bfloat16)
    rest = x - hi.astype(jnp.float32)
    mid, lo = split2(rest)
    return hi, mid, lo


def signed(src, dst, shape, axis):
    at = lax.broadcasted_iota(jnp.int16, shape, axis)
    one, none = jnp.ones(shape, jnp.bfloat16), jnp.zeros(shape, jnp.bfloat16)
    is_src = at == jnp.broadcast_to(src.astype(jnp.int16), shape)
    is_dst = at == jnp.broadcast_to(dst.astype(jnp.int16), shape)
    return jnp.where(is_src, one, jnp.where(is_dst, -one, none))


def halves(x):
    n = x.shape[1] // 2
    return x[:, :n] + x[:, n:]


def dot(a, b):
    return jnp.dot(a, b, preferred_element_type=jnp.float32)


def even_piece(total, most):
    return max(n for n in range(8, most + 1, 8) if total % n == 0)


def slot_copy(src, dst, send_sem, recv_sem, target):
    return pltpu.make_async_remote_copy(
        src_ref=src, dst_ref=dst, send_sem=send_sem, recv_sem=recv_sem,
        device_id=target, device_id_type=pl.DeviceIdType.MESH,
    )


def all_to_all(me, peers, src, dst, send_sem, recv_sem):
    for off in range(1, peers):
        to = lax.rem(me + off, peers)
        slot_copy(src(to), dst.at[me], send_sem.at[off], recv_sem.at[off], {"vtx": to}).start()


def all_to_all_wait(me, peers, src, dst, send_sem, recv_sem):
    for off in range(1, peers):
        to = lax.rem(me + off, peers)
        origin = lax.rem(me + peers - off, peers)
        slot_copy(src(to), dst.at[origin], send_sem.at[off], recv_sem.at[off], {"vtx": to}).wait()


class LineSum:
    lag_total, lag_pass = 2, 4

    def __init__(self, z, pieces, own, outer, inner, mine, result, send_sem, outer_sem, inner_sem):
        self.z, self.pieces, self.own, self.outer, self.inner = z, pieces, own, outer, inner
        self.mine, self.result, self.send_sem = mine, result, send_sem
        self.outer_sem, self.inner_sem = outer_sem, inner_sem
        self.near = 1 + z // 3

    def copy(self, kind, k, src, dst, sem, target):
        rows = pl.ds(*self.pieces[k])
        return slot_copy(src.at[rows], dst.at[rows], self.send_sem.at[kind, k], sem.at[k], {"edg": target})

    def end_copy(self, k):
        return self.copy(0, k, self.own, self.outer, self.outer_sem, self.near)

    def at_end(self, work):
        pl.when((self.z + 1) // 2 % 2 == 0)(work)

    def at_middle(self, work):
        for side in (0, 1):
            pl.when(self.z == 1 + side)(functools.partial(work, side))

    def send_group(self, ks):
        def work():
            for k in ks:
                self.end_copy(k).start()

        self.at_end(work)

    def step(self, side, t):
        own, outer, inner, mine, result = self.own, self.outer, self.inner, self.mine, self.result
        count = len(self.pieces)
        far, peer = 3 * side, 2 - side
        if t < count:
            rows = pl.ds(*self.pieces[t])
            self.copy(1, t, own, outer, self.outer_sem, far).wait_recv()
            if t % 2 != side:
                mine[rows, :] = own[rows, :] + outer[rows, :]
                self.copy(0, t, mine, inner, self.inner_sem, peer).start()
        k = t - self.lag_total
        if 0 <= k < count and k % 2 == side:
            rows = pl.ds(*self.pieces[k])
            self.copy(0, k, mine, inner, self.inner_sem, peer).wait_recv()
            total = (own[rows, :] + outer[rows, :]) + inner[rows, :]
            mine[rows, :] = total
            self.copy(0, k, mine, inner, self.inner_sem, peer).start()
            self.copy(1, k, mine, outer, self.outer_sem, far).start()
            result[rows, :] = total
        k = t - self.lag_pass
        if 0 <= k < count and k % 2 != side:
            rows = pl.ds(*self.pieces[k])
            self.copy(0, k, mine, inner, self.inner_sem, peer).wait_recv()
            self.copy(1, k, inner, outer, self.outer_sem, far).start()
            result[rows, :] = inner[rows, :]

    def pass_group(self, ts):
        def work(side):
            for t in ts:
                self.step(side, t)

        self.at_middle(work)

    def finish(self):
        count = len(self.pieces)

        def end():
            for k in range(count):
                self.end_copy(k).wait_recv()
                rows = pl.ds(*self.pieces[k])
                self.result[rows, :] = self.outer[rows, :]
            for k in range(count):
                self.end_copy(k).wait_send()

        def middle(side):
            for k in range(count):
                self.copy(0, k, self.mine, self.inner, self.inner_sem, 2 - side).wait_send()
                source = self.mine if k % 2 == side else self.inner
                self.copy(1, k, source, self.outer, self.outer_sem, 3 * side).wait_send()

        self.at_end(end)
        self.at_middle(middle)


def stage_kernel(stage, peers, groups, pieces, *refs):
    first, pairs = chebyshev_terms(ITERS)
    last = stage == ITERS - 1
    refs = list(refs)

    def take(n):
        got = refs[:n]
        del refs[:n]
        return got

    g_ref, rows_smem, idx_ref, flt_ref, list_ref, ground_ref = take(6)
    if stage == 0:
        (list8_ref,) = take(1)
    else:
        res_in, dir_in, inv_in = take(3)
        sol_in = take(1)[0] if stage > 1 else dir_in
    if stage == 0:
        dir_ref, res_ref, inv_ref, gout_ref = take(4)
        listed_from = dir_ref
    elif not last:
        dir_ref, res_ref, sol_ref, gout_ref = take(4)
        listed_from = dir_ref
    else:
        sol_ref, gap_ref = take(2)
        listed_from = sol_ref
    own, outer, inner, mine, result, yhalo, back, listed, landed = take(9)
    idxc, fltc, field, part, retb, acc = take(6)
    back_send, back_recv, land_send, land_recv, line_send, outer_sem, inner_sem = take(7)
    if stage == 0:
        flows, degh, dback, dback_send, dback_recv = take(5)
    else:
        flows = g_ref

    me, z = lax.axis_index("vtx"), lax.axis_index("edg")
    slot, columns = back.shape[1], back.shape[2]
    halo_len = peers * slot
    num_rows = ground_ref.shape[0] * LANES
    num_edges = idx_ref.shape[1]
    etile = min(512, num_edges)
    ktile = min(1024, num_edges)

    barrier = pltpu.get_barrier_semaphore()

    def greet(target):
        pl.semaphore_signal(barrier, inc=1, device_id=target, device_id_type=pl.DeviceIdType.MESH)

    for off in range(1, peers):
        greet({"vtx": lax.rem(me + off, peers)})

    @pl.when(z > 0)
    def _():
        greet({"edg": z - 1})

    @pl.when(z < 3)
    def _():
        greet({"edg": z + 1})

    idxc[...] = idx_ref[...].T
    fltc[...] = flt_ref[...].T

    if stage == 0:

        def make_terms(k, _):
            rows = pl.ds(pl.multiple_of(k * etile, etile), etile)
            terms = fltc[rows, 0:1] * g_ref[rows, :].astype(jnp.float32)
            flows[rows, :] = jnp.concatenate(split2(terms), axis=1)
            return 0

        lax.fori_loop(0, num_edges // etile, make_terms, 0)
        weights = flt_ref[1:2, :]
        lane = lax.broadcasted_iota(jnp.int32, (num_edges, LANES), 1)

        def count_up(high, row, column):
            up = lax.broadcasted_iota(jnp.int32, (high, num_edges), 0)
            picked = jnp.where(up == row, weights, 0.0)
            low = jnp.where(lane == column, 1.0, 0.0).astype(jnp.bfloat16)
            parts = dot(jnp.concatenate(split3(picked), axis=0), low)
            return parts[:high] + parts[high : 2 * high] + parts[2 * high :]

        high = num_rows // LANES
        up_rows = -(-high // 16) * 16
        degree_own = count_up(up_rows, idx_ref[2:3, :] // LANES, idxc[:, 2:3] % LANES)
        degree_own += count_up(up_rows, idx_ref[3:4, :] // LANES, idxc[:, 3:4] % LANES)
        own[num_rows:, :] = degree_own[:high]
        degree_far = count_up(-(-peers // 16) * 16, idx_ref[4:5, :], idxc[:, 5:6])
        for q in range(peers):
            degh[q] = jnp.broadcast_to(degree_far[q : q + 1, :], (8, LANES))

    def scatter_rows(at, rows):
        acc[:rows, :] = jnp.zeros((rows, 2 * columns), jnp.float32)

        def body(k, _):
            cols = pl.ds(pl.multiple_of(k * ktile, ktile), ktile)
            pick = signed(idx_ref[0:1, cols] - at, idx_ref[1:2, cols] - at, (rows, ktile), 0)
            acc[:rows, :] += dot(pick, flows[cols, :])
            return 0

        lax.fori_loop(0, num_edges // ktile, body, 0)
        return halves(acc[:rows, :])

    hpiece = even_piece(halo_len, 512)
    for at in range(0, halo_len, hpiece):
        yhalo[at : at + hpiece, :] = scatter_rows(num_rows + at, hpiece)

    pl.semaphore_wait(barrier, peers + (z + 1) // 2 % 2)

    def halo_of(to):
        return yhalo.at[pl.ds(pl.multiple_of(to * slot, 8), slot)]

    def degree_of(to):
        return degh.at[to]

    all_to_all(me, peers, halo_of, back, back_send, back_recv)
    back[me] = yhalo[pl.ds(pl.multiple_of(me * slot, 8), slot), :]
    if stage == 0:
        all_to_all(me, peers, degree_of, dback, dback_send, dback_recv)
        dback[me] = degh[me]

    line = LineSum(z, pieces, own, outer, inner, mine, result, line_send, outer_sem, inner_sem)
    for c, (at, size, ks) in enumerate(groups):
        local_sum = scatter_rows(at, size)
        if c == 0:
            all_to_all_wait(me, peers, halo_of, back, back_send, back_recv)
            retb[...] = jnp.concatenate(split2(back[...].reshape(halo_len, columns)), axis=1)
            if stage == 0:
                all_to_all_wait(me, peers, degree_of, dback, dback_send, dback_recv)
                cols8 = list8_ref[...].T
                up = lax.broadcasted_iota(jnp.int32, (high, LANES), 0)
                lane = lax.broadcasted_iota(jnp.int32, (LANES, LANES), 1)
                for q in range(peers):
                    picked = jnp.where(up == list8_ref[q : q + 1, :] // LANES, dback[q, 0:1, :], 0.0)
                    low = jnp.where(lane == cols8[:, q : q + 1] % LANES, 1.0, 0.0).astype(jnp.bfloat16)
                    parts = dot(jnp.concatenate(split3(picked), axis=0), low)
                    own[num_rows:, :] += parts[:high] + parts[high : 2 * high] + parts[2 * high :]
        row = lax.broadcasted_iota(jnp.int32, (size, halo_len), 0)
        pick = jnp.where(row == list_ref[...] - at, 1.0, 0.0).astype(jnp.bfloat16)
        own[at : at + size, :] = local_sum + halves(dot(pick, retb[...]))
        line.send_group(ks)
        if c > 0:
            line.pass_group(groups[c - 1][2])
    line.pass_group(list(groups[-1][2]) + list(range(len(pieces), len(pieces) + line.lag_pass)))
    line.finish()

    ground_cols = ground_ref[...].T
    if stage == 0:
        inverse = 1.0 / (result[num_rows:, :] + ground_ref[...])
        inv_ref[...] = inverse
    else:
        inverse = inv_in[...]
    inverse_cols = inverse.T
    for at in range(0, num_rows, LANES):
        rows = slice(at, at + LANES)
        j = at // LANES
        inv_col, ground_col = inverse_cols[:, j : j + 1], ground_cols[:, j : j + 1]
        if stage == 0:
            res_ref[rows, :] = result[rows, :]
            shown = first * inv_col * result[rows, :]
            dir_ref[rows, :] = shown
        else:
            keep_coef, push_coef = pairs[stage - 1]
            residual = res_in[rows, :] - (ground_col * dir_in[rows, :] + result[rows, :])
            direction = keep_coef * dir_in[rows, :] + push_coef * inv_col * residual
            total = sol_in[rows, :] + direction
            sol_ref[rows, :] = total
            shown = total
            if not last:
                res_ref[rows, :] = residual
                dir_ref[rows, :] = direction
                shown = direction
        field[rows, :] = jnp.concatenate(split2(shown), axis=1)

    def pick_rows(h, _):
        for q in range(peers):
            listed[q, pl.ds(h, 1), :] = listed_from[pl.ds(rows_smem[q, h], 1), :]
        return 0

    lax.fori_loop(0, slot, pick_rows, 0)

    def listed_of(to):
        return listed.at[to]

    all_to_all(me, peers, listed_of, landed, land_send, land_recv)
    landed[me] = listed[me]

    def gather_near(k, _):
        rows = pl.ds(pl.multiple_of(k * etile, etile), etile)
        d = signed(idxc[rows, 0:1], idxc[rows, 1:2], (etile, num_rows), 1)
        part[rows, :] = halves(dot(d, field[:num_rows, :]))
        return 0

    lax.fori_loop(0, num_edges // etile, gather_near, 0)
    all_to_all_wait(me, peers, listed_of, landed, land_send, land_recv)
    field[num_rows:, :] = jnp.concatenate(split2(landed[...].reshape(halo_len, columns)), axis=1)

    def gather_far(k):
        rows = pl.ds(k * etile, etile)
        d = signed(idxc[rows, 0:1] - num_rows, idxc[rows, 1:2] - num_rows, (etile, halo_len), 1)
        return rows, part[rows, :] + halves(dot(d, field[num_rows:, :]))

    if not last:

        def make_flows(k, _):
            k = pl.multiple_of(k * etile, etile) // etile
            rows, gap = gather_far(k)
            gout_ref[rows, :] = jnp.concatenate(split2(gap * fltc[rows, 1:2]), axis=1)
            return 0

        lax.fori_loop(0, num_edges // etile, make_flows, 0)
    else:
        lane = lax.broadcasted_iota(jnp.int32, (LANES, LANES), 1)
        wide = num_edges // LANES
        for base in range(0, wide, LANES):
            sums = jnp.zeros((LANES, LANES), jnp.float32)
            for k in range(base * LANES // etile, min(wide, base + LANES) * LANES // etile):
                _, gap = gather_far(k)
                square = jnp.sum(gap * gap, axis=1, keepdims=True)
                for i in range(etile // LANES):
                    j = k * (etile // LANES) + i - base
                    sums = jnp.where(lane == j, square[i * LANES : (i + 1) * LANES, :], sums)
            take_rows = min(LANES, wide - base)
            gap_ref[base : base + take_rows, :] = sums.T[:take_rows, :]


def run_stage(stage, peers, slot, num_rows, columns, num_edges, operands):
    high = num_rows // LANES
    extra = high if stage == 0 else 0
    size, big = 128, 512
    pieces = [(at, size) for at in range(0, num_rows, size)]
    groups = [[at, big, list(range(at // size, (at + big) // size))] for at in range(0, num_rows, big)]
    if extra:
        groups[-1][2].append(len(pieces))
        pieces.append((num_rows, extra))
    count = len(pieces)
    f32, bf16, i32 = jnp.float32, jnp.bfloat16, jnp.int32
    halo_len = peers * slot
    field = jax.ShapeDtypeStruct((num_rows, columns), f32)
    flows = jax.ShapeDtypeStruct((num_edges, 2 * columns), bf16)
    if stage == 0:
        outs = [field, field, jax.ShapeDtypeStruct((high, LANES), f32), flows]
    elif stage < ITERS - 1:
        outs = [field, field, field, flows]
    else:
        outs = [field, jax.ShapeDtypeStruct((num_edges // LANES, LANES), f32)]
    vmem = pl.BlockSpec(memory_space=pltpu.VMEM)
    in_specs = [vmem] * len(operands)
    in_specs[1] = pl.BlockSpec(memory_space=pltpu.SMEM)
    dma = pltpu.SemaphoreType.DMA
    buffer = pltpu.VMEM((num_rows + extra, columns), f32)
    halo = pltpu.VMEM((peers, slot, columns), f32)
    scratch = [buffer] * 5 + [pltpu.VMEM((halo_len, columns), f32)] + [halo] * 3
    scratch += [pltpu.VMEM((num_edges, 8), i32), pltpu.VMEM((num_edges, 8), f32)]
    scratch += [pltpu.VMEM((num_rows + halo_len, 2 * columns), bf16), pltpu.VMEM((num_edges, columns), f32)]
    scratch += [pltpu.VMEM((halo_len, 2 * columns), bf16), pltpu.VMEM((big, 2 * columns), f32)]
    scratch += [dma((peers,))] * 4 + [dma((2, count)), dma((count,)), dma((count,))]
    if stage == 0:
        scratch += [pltpu.VMEM((num_edges, 2 * columns), bf16)]
        scratch += [pltpu.VMEM((peers, 8, LANES), f32)] * 2 + [dma((peers,)), dma((peers,))]
    return pl.pallas_call(
        functools.partial(stage_kernel, stage, peers, groups, pieces),
        in_specs=in_specs,
        out_specs=[vmem] * len(outs),
        out_shape=outs,
        scratch_shapes=scratch,
        compiler_params=pltpu.CompilerParams(collective_id=stage, has_side_effects=True, vmem_limit_bytes=VMEM_LIMIT),
        name="stage%d" % stage,
    )(*operands)


def local(sketch_cols, edge_weight, ground, src_local, dst_index, send_rows, edge_count):
    blocks = lax.axis_size("vtx")
    num_rows = ground.shape[0]
    num_edges = edge_weight.shape[0]
    slot_width = send_rows.shape[2]
    columns = sketch_cols.shape[1]
    row_lists = send_rows[0]
    live_mask = (jnp.arange(num_edges, dtype=jnp.int32) < edge_count[0]).astype(jnp.float32)
    weight_live = edge_weight * live_mask
    root_live = jnp.sqrt(edge_weight) * live_mask
    loop = src_local == dst_index
    slots = dst_index - num_rows
    peer = jnp.where(slots < 0, -1, slots // slot_width)
    within = jnp.where(slots < 0, -1, slots % slot_width)
    idx = jnp.stack(
        [jnp.where(loop, -1, src_local), jnp.where(loop, -1, dst_index), src_local, dst_index, peer, within, loop.astype(jnp.int32), peer]
    )
    zero = jnp.zeros_like(root_live)
    flt = jnp.stack([root_live, weight_live] + [zero] * 6)
    flat_row = row_lists.reshape(1, -1)
    ground_rows = ground.reshape(num_rows // LANES, LANES)
    list8 = jnp.pad(row_lists, ((0, 0), (0, LANES - slot_width)), constant_values=-1)
    stage = functools.partial(
        run_stage, peers=blocks, slot=slot_width, num_rows=num_rows, columns=columns, num_edges=num_edges
    )
    common = (row_lists, idx, flt, flat_row, ground_rows)
    direction, residual, inverse, flows = stage(0, operands=(sketch_cols,) + common + (list8,))
    state = (residual, direction, inverse)
    for step_idx in range(1, ITERS):
        if step_idx < ITERS - 1:
            direction, residual, solution, flows = stage(step_idx, operands=(flows,) + common + state)
            state = (residual, direction, inverse, solution)
        else:
            solution, gaps = stage(step_idx, operands=(flows,) + common + state)
    resistance = live_mask * gaps.reshape(-1) / columns
    return (solution, resistance)


def solution(mesh):
    in_specs = (
        P(("vtx", "edg"), None),
        P(("vtx", "edg")),
        P("vtx"),
        P(("vtx", "edg")),
        P(("vtx", "edg")),
        P(("vtx", "edg"), None, None),
        P(("vtx", "edg")),
    )
    out_specs = (P("vtx", None), P(("vtx", "edg")))
    return jax.shard_map(local, mesh=mesh, in_specs=in_specs, out_specs=out_specs, check_vma=False)
```

profile of v0, /device:TPU:0, one launch (start us, length us, event | category | flops | bytes accessed | tf_op | source)
XLA Modules:
  0.0 199.4 jit_solution(2013895475913658024)
XLA Ops:
  1.3 0.1 pad.7.clone
  1.4 0.1 pad.8.clone
  1.4 1.3 reshape_squeeze.3.refs_4_
  2.7 1.3 pad.4.refs_6_
  4.0 0.7 fusion.5
  4.8 0.7 sqrt_select_fusion
  5.5 0.8 fusion.1
  6.3 1.6 stack.51.refs_2_
  7.8 0.7 maximum_maximum_fusion.refs_3_
  8.6 68.0 %stage0.1 = (f32[2048,128]{1,0:T(8,128)}, f32[2048,128]{1,0:T(8,128)}, f32[16,128]{1,0:T(8,128)}, bf16[4096,256]{1,0:T(8,128)(2,1)}) custom-call(bf16[4096,128]{1,0:T(8,128)(2,1)} %refs_0_.1, s32[8,48]{1,0:T(8,128)} %bitcast.23, s32[8,4096]{1,0:T(8,128)} %stack.51.refs_2_, f32[8,4096]{1,0:T(8,128)} %maximum_maximum_fusion.refs_3_, ...), custom_call_target="tpu_custom_call" | custom-call | tf_op jit(solution)/shard_map/stage0/pallas_call | solution.py:426
  76.6 59.9 %stage1.1 = (f32[2048,128]{1,0:T(8,128)}, f32[2048,128]{1,0:T(8,128)}, f32[2048,128]{1,0:T(8,128)}, bf16[4096,256]{1,0:T(8,128)(2,1)}) custom-call(bf16[4096,256]{1,0:T(8,128)(2,1)} %get-tuple-element.12.refs_0_, s32[8,48]{1,0:T(8,128)} %bitcast.24, s32[8,4096]{1,0:T(8,128)} %stack.51.refs_2_, f32[8,4096]{1,0:T(8,128)} %maximum_maximum_fusion.refs_3_, ...), custom_call_target="tpu_custom_call" | custom-call | tf_op jit(solution)/shard_map/stage1/pallas_call | solution.py:426
  136.5 59.3 %stage2.1 = (f32[2048,128]{1,0:T(8,128)}, f32[32,128]{1,0:T(8,128)}) custom-call(bf16[4096,256]{1,0:T(8,128)(2,1)} %get-tuple-element.16.refs_0_, s32[8,48]{1,0:T(8,128)} %bitcast.25, s32[8,4096]{1,0:T(8,128)} %stack.51.refs_2_, f32[8,4096]{1,0:T(8,128)} %maximum_maximum_fusion.refs_3_, s32[1,384]{1,0:T(1,128)} %reshape_squeeze.3.refs_4_, ...), custom_call_target="tpu_custom_call" | custom-call | tf_op jit(solution)/shard_map/stage2/pallas_call | solution.py:426
  195.8 1.3 fusion.2
  197.1 2.3 %copy.11 = f32[2048,128]{1,0:T(8,128)} copy(f32[2048,128]{1,0:T(8,128)} %get-tuple-element.32) | data formatting | bytes 2097152
  (2 shorter events, 0.0 us)
where the time goes:
time: 200 us; the launch traced here: 199 us
  Pallas kernels  187 us (94%)
  local copies, waits for them, and re-layouts  6.57 us (3%)
  other arithmetic  4.29 us (2%)
    pallas_call x3, Pallas kernels, run_stage(): pl.pallas_call(functools.partial(stage_kernel, stage, peers, groups, piec...  187 us

commit v1 on v0

v1 whole, which is shorter than its diff:
```python
import functools

import jax
import jax.numpy as jnp
from jax import lax
from jax.experimental import pallas as pl
from jax.experimental.pallas import tpu as pltpu
from jax.sharding import PartitionSpec as P

ITERS = 3

lam_low = 0.05
lam_high = 2.0
LANES = 128
VMEM_LIMIT = 62 * 1024 * 1024
GROUP = 512
PIECE = 128
LAG = 3


def chebyshev_terms(steps):
    centre = (lam_high + lam_low) / 2.0
    half_width = (lam_high - lam_low) / 2.0
    sigma_val = centre / half_width
    rho_prev = 1.0 / sigma_val
    pairs = []
    for count_idx in range(steps - 1):
        rho_next = 1.0 / (2.0 * sigma_val - rho_prev)
        pairs.append((rho_next * rho_prev, 2.0 * rho_next / half_width))
        rho_prev = rho_next
    return (1.0 / centre, pairs)


def split2(x):
    hi = x.astype(jnp.bfloat16)
    lo = (x - hi.astype(jnp.float32)).astype(jnp.bfloat16)
    return hi, lo


def split3(x):
    hi = x.astype(jnp.bfloat16)
    rest = x - hi.astype(jnp.float32)
    mid, lo = split2(rest)
    return hi, mid, lo


def pair(x):
    return jnp.concatenate(split2(x), axis=1)


def halves(x):
    n = x.shape[1] // 2
    return x[:, :n] + x[:, n:]


def dot(a, b):
    return jnp.dot(a, b, preferred_element_type=jnp.float32)


def signed(is_src, is_dst):
    one, none = jnp.ones(is_src.shape, jnp.bfloat16), jnp.zeros(is_src.shape, jnp.bfloat16)
    return jnp.where(is_src, one, jnp.where(is_dst, -one, none))


def one_hot(match):
    return jnp.where(match, jnp.ones(match.shape, jnp.bfloat16), jnp.zeros(match.shape, jnp.bfloat16))


def short(x, shape):
    return jnp.broadcast_to(jnp.asarray(x, jnp.int32), shape).astype(jnp.int16)


def down_rows(row, at, rows):
    shape = (rows, row.shape[1])
    return lax.broadcasted_iota(jnp.int16, shape, 0) == jnp.broadcast_to((row - at).astype(jnp.int16), shape)


def along_lanes(spread, at, width):
    parts = []
    lane = lax.broadcasted_iota(jnp.int16, spread.shape, 1)
    for off in range(0, width, LANES):
        parts.append(lane + short(at + off, spread.shape) == spread)
    return parts


def even_piece(total, most):
    return max(n for n in range(8, most + 1, 8) if total % n == 0)


def remote(src, dst, send_sem, recv_sem, target):
    return pltpu.make_async_remote_copy(
        src_ref=src, dst_ref=dst, send_sem=send_sem, recv_sem=recv_sem,
        device_id=target, device_id_type=pl.DeviceIdType.MESH,
    )


def exchange(me, peers, src, dst, send_sem, recv_sem):
    def start(off, _):
        to = lax.rem(me + off, peers)
        remote(src(to), dst.at[me], send_sem.at[off], recv_sem.at[off], {"vtx": to}).start()
        return 0

    lax.fori_loop(1, peers, start, 0)


def exchange_wait(me, peers, src, dst, send_sem, recv_sem):
    def wait(off, _):
        to = lax.rem(me + off, peers)
        origin = lax.rem(me + peers - off, peers)
        remote(src(to), dst.at[origin], send_sem.at[off], recv_sem.at[off], {"vtx": to}).wait()
        return 0

    lax.fori_loop(1, peers, wait, 0)


def kernel(
    peers, sketch_ref, weight_ref, ground_ref, src_ref, dst_ref, list_ref, count_ref, sol_ref, gap_ref,
    rowf, srow, dstb, wide, wb, listb, listrow, groundb, invb, res, dirn, field, part, acc, retb,
    flows, own, outer, inner, mine, total, yhalo, back, listed, landed, mask, list8, list8b, list8row,
    degown, degouter, deginner, degmine, degtotal, degh, dback,
    back_sem, land_sem, deg_sem, line_sem, degline_sem,
):
    first, pairs = chebyshev_terms(ITERS)
    me, z = lax.axis_index("vtx"), lax.axis_index("edg")
    slot, columns = back.shape[2], back.shape[3]
    halo_len = peers * slot
    wide_rows = src_ref.shape[0]
    num_edges = wide_rows * LANES
    num_rows = sol_ref.shape[0]
    high = num_rows // LANES
    ktile = min(1024, num_edges)
    etile = 512
    quarter = num_edges // 4
    groups = num_rows // GROUP
    per = GROUP // PIECE
    count = num_rows // PIECE
    middle = (z + 1) // 2 % 2 == 1
    at_end = (z + 1) // 2 % 2 == 0
    near, far, peer = {"edg": 1 + z // 3}, {"edg": 3 * (z // 2)}, {"edg": 3 - z}
    f32, bf16, i32 = jnp.float32, jnp.bfloat16, jnp.int32

    barrier = pltpu.get_barrier_semaphore()

    def greet(target):
        pl.semaphore_signal(barrier, inc=1, device_id=target, device_id_type=pl.DeviceIdType.MESH)

    def greet_peer(off, _):
        greet({"vtx": lax.rem(me + off, peers)})
        return 0

    lax.fori_loop(1, peers, greet_peer, 0)

    @pl.when(at_end)
    def _():
        greet(near)

    @pl.when(middle)
    def _():
        greet(far)
        greet(peer)

    shape = (wide_rows, LANES)
    position = lax.broadcasted_iota(i32, shape, 0) * LANES + lax.broadcasted_iota(i32, shape, 1)
    live = position < count_ref[0]
    src, dst = src_ref[...], dst_ref[...]
    slots = dst - num_rows
    weight = jnp.where(live, weight_ref[...], 0.0)
    apart = jnp.logical_and(live, src != dst)
    held = jnp.where(apart, weight_ref[...], 0.0)
    root = jnp.sqrt(held)
    mask[...] = jnp.where(apart, 1.0, 0.0)
    peer_of = jnp.where(slots < 0, -1, slots // slot)
    within = jnp.where(slots < 0, -1, slots % slot)
    along = [src, dst, src // LANES, dst // LANES, peer_of]
    for k in range(wide_rows):
        cols = slice(k * LANES, (k + 1) * LANES)
        for row, value in enumerate(along):
            rowf[row : row + 1, cols] = value[k : k + 1, :]
        wide[0:1, cols] = weight[k : k + 1, :]
    src_t, dst_t, within_t = src.T, dst.T, within.T
    held_t, root_t = held.T, root.T
    for k in range(wide_rows):
        rows = slice(k * LANES, (k + 1) * LANES)
        block = (LANES, LANES)
        srow[rows, :] = short(src_t[:, k : k + 1], block)
        dstb[rows, :] = short(dst_t[:, k : k + 1], block)
        wb[rows, :] = jnp.broadcast_to(held_t[:, k : k + 1], block)
    srcb = srow

    lane_e = lax.broadcasted_iota(jnp.int16, (num_edges, LANES), 1)

    def count_up(rows, row, low):
        weights = wide[0:1, :]
        up = lax.broadcasted_iota(i32, (rows, num_edges), 0)
        picked = jnp.where(up == row, weights, 0.0)
        parts = dot(jnp.concatenate(split3(picked), axis=0), low)
        return parts[:rows] + parts[rows : 2 * rows] + parts[2 * rows :]

    for k in range(wide_rows):
        rows = slice(k * LANES, (k + 1) * LANES)
        match = lax.broadcasted_iota(jnp.int16, (LANES, LANES), 1) == short(within_t[:, k : k + 1], (LANES, LANES))
        flows[rows, :LANES] = one_hot(match)
    degree_far = count_up(-(-peers // 16) * 16, rowf[4:5, :], flows[:, :LANES])
    for q in range(peers):
        degh[q] = jnp.broadcast_to(degree_far[q : q + 1, :], (8, LANES))

    pl.semaphore_wait(barrier, peers + jnp.where(middle, 1, 0))

    def degree_of(to):
        return degh.at[to]

    exchange(me, peers, degree_of, dback, deg_sem.at[0], deg_sem.at[1])
    dback[me] = degh[me]

    for k in range(wide_rows):
        rows = slice(k * LANES, (k + 1) * LANES)
        flows[rows, :] = pair(-(root_t[:, k : k + 1] * sketch_ref[rows, :].astype(f32)))

    list8[...] = jnp.full(list8.shape, -1, i32)
    list8[:peers, :slot] = list_ref[...]
    list_t = list8[...].T
    for q in range(peers):
        spread = jnp.broadcast_to(list_t[:, q : q + 1], (LANES, LANES))
        list8b[q * LANES : (q + 1) * LANES, :] = spread.astype(jnp.int16)
        list8row[0:1, q * LANES : (q + 1) * LANES] = list8[q : q + 1, :]
        listb[q * slot : (q + 1) * slot, :] = spread[:slot]
    for at in range(0, halo_len, LANES):
        listrow[0:1, at : at + LANES] = listb[at : at + LANES, :].T[0:1, :]

    ground_t = ground_ref[...].T
    for j in range(high):
        rows = slice(j * LANES, (j + 1) * LANES)
        groundb[rows, :] = jnp.broadcast_to(ground_t[:, j : j + 1], (LANES, LANES))
    for ref in (res, dirn, sol_ref, part):
        ref[...] = jnp.zeros(ref.shape, f32)

    def scatter_rows(at, rows):
        acc[:rows, :] = jnp.zeros((rows, 2 * columns), f32)

        def body(k, _):
            cols = pl.ds(pl.multiple_of(k * ktile, ktile), ktile)
            pick = signed(down_rows(rowf[0:1, cols], at, rows), down_rows(rowf[1:2, cols], at, rows))
            acc[:rows, :] += dot(pick, flows[cols, :])
            return 0

        lax.fori_loop(0, num_edges // ktile, body, 0)
        return halves(acc[:rows, :])

    def edge_hots(rows, at, width):
        hots = zip(along_lanes(srcb[rows, :], at, width), along_lanes(dstb[rows, :], at, width))
        return jnp.concatenate([signed(a, b) for a, b in hots], axis=1)

    def gather_near(group, q):
        for off in range(0, quarter, etile):
            rows = pl.ds(pl.multiple_of(q * quarter + off, etile), etile)
            base = pl.multiple_of(group * GROUP, GROUP)
            hots = edge_hots(rows, base, GROUP)
            part[rows, :] += halves(dot(hots, field[pl.ds(base, GROUP), :]))

    def own_degree():
        low = one_hot(jnp.bitwise_and(srcb[...], jnp.int16(LANES - 1)) == lane_e)
        rows = -(-high // 16) * 16
        got = count_up(rows, rowf[2:3, :], low)
        low = one_hot(jnp.bitwise_and(dstb[...], jnp.int16(LANES - 1)) == lane_e)
        got += count_up(rows, rowf[3:4, :], low)
        up = lax.broadcasted_iota(i32, (rows, peers * LANES), 0)
        for q in range(peers):
            wide[0:1, q * LANES : (q + 1) * LANES] = dback[q, 0:1, :]
        picked = jnp.where(up == list8row[...] // LANES, wide[0:1, : peers * LANES], 0.0)
        lane = lax.broadcasted_iota(jnp.int16, (peers * LANES, LANES), 1)
        low = one_hot(jnp.bitwise_and(list8b[...], jnp.int16(LANES - 1)) == lane)
        parts = dot(jnp.concatenate(split3(picked), axis=0), low)
        got += parts[:rows] + parts[rows : 2 * rows] + parts[2 * rows :]
        degown[...] = got[:high]

    def degree_copy(kind, src, dst, target):
        return remote(src, dst, degline_sem.at[0, kind], degline_sem.at[1, kind], target)

    hpiece = even_piece(halo_len, 512)

    def stage(s, _):
        begin, last = s == 0, s == ITERS - 1
        keep, push = jnp.float32(0.0), jnp.float32(first)
        for at, (k_coef, p_coef) in enumerate(pairs):
            keep = jnp.where(s == at + 1, jnp.float32(k_coef), keep)
            push = jnp.where(s == at + 1, jnp.float32(p_coef), push)

        def line_copy(kind, k, src, dst, target):
            rows = pl.ds(pl.multiple_of(k * PIECE, PIECE), PIECE)
            return remote(
                src.at[s, rows], dst.at[s, rows], line_sem.at[0, s, kind, k], line_sem.at[1, s, kind, k], target
            )

        def to_middle(k):
            return line_copy(0, k, own, outer, near)

        def to_peer(k):
            return line_copy(1, k, mine, inner, peer)

        def to_end(k):
            return line_copy(2, k, total, total, far)

        def from_end(k):
            return line_copy(0, k, own, outer, far)

        def from_middle(k):
            return line_copy(2, k, total, total, near)

        def piece_rows(k):
            return pl.ds(pl.multiple_of(k * PIECE, PIECE), PIECE)

        def pass_partial(k):
            rows = piece_rows(k)
            from_end(k).wait_recv()
            mine[s, rows, :] = own[s, rows, :] + outer[s, rows, :]
            to_peer(k).start()

        def pass_total(k):
            rows = piece_rows(k)
            to_peer(k).wait_recv()
            total[s, rows, :] = mine[s, rows, :] + inner[s, rows, :]
            to_end(k).start()

        for at in range(0, halo_len, hpiece):
            yhalo[s, at : at + hpiece, :] = scatter_rows(num_rows + at, hpiece)

        def halo_of(to):
            return yhalo.at[s, pl.ds(pl.multiple_of(to * slot, 8), slot)]

        back_args = (me, peers, halo_of, back.at[s], back_sem.at[0, s], back_sem.at[1, s])
        exchange(*back_args)
        back[s, me] = yhalo[s, pl.ds(pl.multiple_of(me * slot, 8), slot), :]

        def group_rows(c, _):
            at = pl.multiple_of(c * GROUP, GROUP)
            local = scatter_rows(at, GROUP)

            @pl.when(jnp.logical_and(begin, c == 0))
            def _():
                exchange_wait(me, peers, degree_of, dback, deg_sem.at[0], deg_sem.at[1])
                own_degree()

            @pl.when(c == 0)
            def _():
                exchange_wait(*back_args)
                retb[...] = pair(back[s].reshape(halo_len, columns))

            @pl.when(jnp.logical_and(begin, c == 0))
            def _():
                @pl.when(at_end)
                def _():
                    degree_copy(0, degown, degouter, near).start()

            pick = one_hot(down_rows(listrow[...], at, GROUP))
            own[s, pl.ds(at, GROUP), :] = local + halves(dot(pick, retb[...]))

            @pl.when(at_end)
            def _():
                for j in range(per):
                    to_middle(c * per + j).start()

            @pl.when(jnp.logical_and(middle, c == groups - 2))
            def _():
                @pl.when(begin)
                def _():
                    degree_copy(0, degown, degouter, far).wait_recv()
                    degmine[...] = degown[...] + degouter[...]
                    degree_copy(1, degmine, deginner, peer).start()

                for k in range(LAG):
                    pass_partial(k)

            return 0

        lax.fori_loop(0, groups, group_rows, 0)

        @pl.when(begin)
        def _():
            @pl.when(middle)
            def _():
                degree_copy(1, degmine, deginner, peer).wait_recv()
                degtotal[...] = degmine[...] + deginner[...]
                degree_copy(2, degtotal, degtotal, far).start()

            @pl.when(at_end)
            def _():
                degree_copy(2, degtotal, degtotal, near).wait_recv()

            inverse_t = (1.0 / (degtotal[...] + ground_ref[...])).T
            for j in range(high):
                rows = slice(j * LANES, (j + 1) * LANES)
                invb[rows, :] = jnp.broadcast_to(inverse_t[:, j : j + 1], (LANES, LANES))

        def step(k, _):
            rows = piece_rows(k)

            @pl.when(middle)
            def _():
                @pl.when(k + LAG < count)
                def _():
                    pass_partial(k + LAG)

                pass_total(k)

            @pl.when(at_end)
            def _():
                from_middle(k).wait_recv()

            old = dirn[rows, :]
            residual = res[rows, :] - (groundb[rows, :] * old + total[s, rows, :])
            direction = keep * old + push * invb[rows, :] * residual
            shown = sol_ref[rows, :] + direction
            res[rows, :] = residual
            dirn[rows, :] = direction
            sol_ref[rows, :] = shown
            field[rows, :] = pair(jnp.where(last, shown, direction))
            group, j = k // per, lax.rem(k, per)

            @pl.when(j == per - 1)
            def _():
                base = pl.multiple_of(group * GROUP, GROUP)
                for at in range(0, halo_len, hpiece):
                    spread = listb[at : at + hpiece, :].astype(jnp.int16)
                    hots = jnp.concatenate([one_hot(m) for m in along_lanes(spread, base, GROUP)], axis=1)
                    got = halves(dot(hots, field[pl.ds(base, GROUP), :]))
                    listed[s, at : at + hpiece, :] = jnp.where(group == 0, got, listed[s, at : at + hpiece, :] + got)

            @pl.when(group > 0)
            def _():
                gather_near(group - 1, j)

            return 0

        lax.fori_loop(0, count, step, 0)

        def listed_of(to):
            return listed.at[s, pl.ds(pl.multiple_of(to * slot, 8), slot)]

        land_args = (me, peers, listed_of, landed.at[s], land_sem.at[0, s], land_sem.at[1, s])
        exchange(*land_args)
        landed[s, me] = listed[s, pl.ds(pl.multiple_of(me * slot, 8), slot), :]

        def near_tail(q, _):
            gather_near(groups - 1, q)
            return 0

        lax.fori_loop(0, 4, near_tail, 0)
        exchange_wait(*land_args)
        field[num_rows:, :] = pair(landed[s].reshape(halo_len, columns))

        def gather_far(k):
            rows = pl.ds(pl.multiple_of(k * etile, etile), etile)
            gap = part[rows, :] + halves(dot(edge_hots(rows, num_rows, halo_len), field[num_rows:, :]))
            part[rows, :] = jnp.zeros(gap.shape, f32)
            return rows, gap

        @pl.when(jnp.logical_not(last))
        def _():
            def make_flows(k, _):
                rows, gap = gather_far(k)
                flows[rows, :] = pair(gap * wb[rows, :])
                return 0

            lax.fori_loop(0, num_edges // etile, make_flows, 0)

        @pl.when(last)
        def _():
            def make_gaps(k, _):
                rows, gap = gather_far(k)
                square = gap * gap
                for i in range(etile // LANES):
                    block = square[i * LANES : (i + 1) * LANES, :].T
                    row = pl.ds(k * (etile // LANES) + i, 1)
                    gap_ref[row, :] = mask[row, :] * jnp.sum(block, axis=0, keepdims=True) / columns
                return 0

            lax.fori_loop(0, num_edges // etile, make_gaps, 0)

        def line_done(k, _):
            @pl.when(at_end)
            def _():
                to_middle(k).wait_send()

            @pl.when(middle)
            def _():
                to_peer(k).wait_send()
                to_end(k).wait_send()

            return 0

        lax.fori_loop(0, count, line_done, 0)
        return 0

    lax.fori_loop(0, ITERS, stage, 0)

    @pl.when(at_end)
    def _():
        degree_copy(0, degown, degouter, near).wait_send()

    @pl.when(middle)
    def _():
        degree_copy(1, degmine, deginner, peer).wait_send()
        degree_copy(2, degtotal, degtotal, far).wait_send()


def local(sketch_cols, edge_weight, ground, src_local, dst_index, send_rows, edge_count):
    peers = lax.axis_size("vtx")
    num_rows, num_edges = ground.shape[0], edge_weight.shape[0]
    slot, columns = send_rows.shape[2], sketch_cols.shape[1]
    halo_len, high, wide_rows = peers * slot, num_rows // LANES, num_edges // LANES
    count = num_rows // PIECE
    f32, bf16, i32, i16 = jnp.float32, jnp.bfloat16, jnp.int32, jnp.int16
    vmem, dma = pltpu.VMEM, pltpu.SemaphoreType.DMA
    peers8 = -(-peers // 8) * 8
    halo = vmem((ITERS, peers, slot, columns), f32)
    flat_halo = vmem((ITERS, halo_len, columns), f32)
    rows_f32 = vmem((num_rows, columns), f32)
    line = vmem((ITERS, num_rows, columns), f32)
    small = vmem((high, LANES), f32)
    spread = vmem((num_edges, LANES), i16)
    scratch = [
        vmem((8, num_edges), i32), spread, spread,
        vmem((8, max(num_edges, peers * LANES)), f32), vmem((num_edges, LANES), f32),
        vmem((halo_len, LANES), i32), vmem((1, halo_len), i32),
        rows_f32, rows_f32, rows_f32, rows_f32,
        vmem((num_rows + halo_len, 2 * columns), bf16), vmem((num_edges, columns), f32),
        vmem((GROUP, 2 * columns), f32), vmem((halo_len, 2 * columns), bf16),
        vmem((num_edges, 2 * columns), bf16), line, line, line, line, line,
        flat_halo, halo, flat_halo, halo,
        vmem((wide_rows, LANES), f32), vmem((peers8, LANES), i32),
        vmem((peers * LANES, LANES), i16), vmem((1, peers * LANES), i32),
        small, small, small, small, small, vmem((peers, 8, LANES), f32), vmem((peers, 8, LANES), f32),
        dma((2, ITERS, peers)), dma((2, ITERS, peers)), dma((2, peers)), dma((2, ITERS, 3, count)), dma((2, 3)),
    ]
    in_vmem = pl.BlockSpec(memory_space=pltpu.VMEM)
    solution, gaps = pl.pallas_call(
        functools.partial(kernel, peers),
        in_specs=[in_vmem] * 6 + [pl.BlockSpec(memory_space=pltpu.SMEM)],
        out_specs=[in_vmem] * 2,
        out_shape=[jax.ShapeDtypeStruct((num_rows, columns), f32), jax.ShapeDtypeStruct((wide_rows, LANES), f32)],
        scratch_shapes=scratch,
        compiler_params=pltpu.CompilerParams(collective_id=0, has_side_effects=True, vmem_limit_bytes=VMEM_LIMIT),
        name="sketch",
    )(
        sketch_cols, edge_weight.reshape(wide_rows, LANES), ground.reshape(high, LANES),
        src_local.reshape(wide_rows, LANES), dst_index.reshape(wide_rows, LANES), send_rows[0], edge_count,
    )
    return solution, gaps.reshape(-1)


def solution(mesh):
    in_specs = (
        P(("vtx", "edg"), None),
        P(("vtx", "edg")),
        P("vtx"),
        P(("vtx", "edg")),
        P(("vtx", "edg")),
        P(("vtx", "edg"), None, None),
        P(("vtx", "edg")),
    )
    out_specs = (P("vtx", None), P(("vtx", "edg")))
    return jax.shard_map(local, mesh=mesh, in_specs=in_specs, out_specs=out_specs, check_vma=False)
```

time: 200 us -> 155 us (0.78)
  Pallas kernels: 187 us -> 151 us
  other arithmetic: 4.29 us -> 0 us
  local copies, waits for them, and re-layouts: 6.57 us -> 2.88 us
    pallas_call x3 -> x1, Pallas kernels: 187 us -> 151 us  [local(): pl.pallas_call(functools.partial(kernel, peers), in_specs=[in_vmem] * 6 +...]
    another operation x6 -> x0, local copies, waits for them, and re-layouts: 3.03 us -> none  [the longest x1 1.57 us: local(): jnp.stack([jnp.where(loop, -1, src_local), jnp.where(loop, -1, dst_index)...]
where the time goes in v1:
time: 155 us
  Pallas kernels  151 us (97%)
  local copies, waits for them, and re-layouts  2.88 us (2%)
    pallas_call x1, Pallas kernels, local(): pl.pallas_call(functools.partial(kernel, peers), in_specs=[in_vmem] * 6 +...  151 us

profile of v1, /device:TPU:0, one launch (start us, length us, event | category | flops | bytes accessed | tf_op | source)
XLA Modules:
  0.0 155.2 jit_solution(10852553952311944903)
XLA Ops:
  1.3 151.0 %sketch.1 = (f32[2048,128]{1,0:T(8,128)}, f32[32,128]{1,0:T(8,128)}) custom-call(bf16[4096,128]{1,0:T(8,128)(2,1)} %sketch_ref.1, f32[32,128]{1,0:T(8,128)} %bitcast.6, f32[16,128]{1,0:T(8,128)} %bitcast.10, s32[32,128]{1,0:T(8,128)} %bitcast.7, s32[32,128]{1,0:T(8,128)} %bitcast.8, s32[8,48]{1,0:T(8,128)} %bitcast.11, s32[1]{0:T(128)S(6)} %copy.11.count_ref), custom_call_target="tpu_custom_call" | custom-call | tf_op jit(solution)/shard_map/sketch/pallas_call | solution.py:536
  152.3 0.0 copy-start
  152.3 2.3 %copy.12 = f32[2048,128]{1,0:T(8,128)} copy(f32[2048,128]{1,0:T(8,128)} %get-tuple-element.8) | data formatting | bytes 2097152
  154.5 0.0 copy-done
  154.5 0.6 copy.13
Async XLA Ops:
  152.3 2.3 %copy-start = (f32[32,128]{1,0:T(8,128)S(1)}, f32[32,128]{1,0:T(8,128)}, u32[]{:S(2)}) copy-start(f32[32,128]{1,0:T(8,128)} %get-tuple-element.5) | copy-start | bytes 49156

commit v2 on v1

--- a/solution.py
+++ b/solution.py
@@ -57,6 +57,10 @@
     return jnp.dot(a, b, preferred_element_type=jnp.float32)
 
 
+def dot_lanes(a, b):
+    return lax.dot_general(a, b, (((1,), (1,)), ((), ())), preferred_element_type=jnp.float32)
+
+
 def signed(is_src, is_dst):
     one, none = jnp.ones(is_src.shape, jnp.bfloat16), jnp.zeros(is_src.shape, jnp.bfloat16)
     return jnp.where(is_src, one, jnp.where(is_dst, -one, none))
@@ -115,8 +119,8 @@
 
 def kernel(
     peers, sketch_ref, weight_ref, ground_ref, src_ref, dst_ref, list_ref, count_ref, sol_ref, gap_ref,
-    rowf, srow, dstb, wide, wb, listb, listrow, groundb, invb, res, dirn, field, part, acc, retb,
-    flows, own, outer, inner, mine, total, yhalo, back, listed, landed, mask, list8, list8b, list8row,
+    rowf, srcb, dstb, wide, wb, listb, listrow, groundb, invb, res, dirn, field, part, acc, retb,
+    flows, own, outer, inner, mine, total, yhalo, back, listed, landed, mask, list8, list8row,
     degown, degouter, deginner, degmine, degtotal, degh, dback,
     back_sem, land_sem, deg_sem, line_sem, degline_sem,
 ):
@@ -129,7 +133,7 @@
     num_rows = sol_ref.shape[0]
     high = num_rows // LANES
     ktile = min(1024, num_edges)
-    etile = 512
+    etile = 1024
     quarter = num_edges // 4
     groups = num_rows // GROUP
     per = GROUP // PIECE
@@ -171,68 +175,54 @@
     mask[...] = jnp.where(apart, 1.0, 0.0)
     peer_of = jnp.where(slots < 0, -1, slots // slot)
     within = jnp.where(slots < 0, -1, slots % slot)
-    along = [src, dst, src // LANES, dst // LANES, peer_of]
     for k in range(wide_rows):
         cols = slice(k * LANES, (k + 1) * LANES)
-        for row, value in enumerate(along):
-            rowf[row : row + 1, cols] = value[k : k + 1, :]
+        rowf[0:1, cols] = src[k : k + 1, :]
+        rowf[1:2, cols] = dst[k : k + 1, :]
+        rowf[2:3, cols] = peer_of[k : k + 1, :]
+        rowf[3:4, cols] = within[k : k + 1, :]
         wide[0:1, cols] = weight[k : k + 1, :]
-    src_t, dst_t, within_t = src.T, dst.T, within.T
-    held_t, root_t = held.T, root.T
-    for k in range(wide_rows):
-        rows = slice(k * LANES, (k + 1) * LANES)
-        block = (LANES, LANES)
-        srow[rows, :] = short(src_t[:, k : k + 1], block)
-        dstb[rows, :] = short(dst_t[:, k : k + 1], block)
-        wb[rows, :] = jnp.broadcast_to(held_t[:, k : k + 1], block)
-    srcb = srow
-
-    lane_e = lax.broadcasted_iota(jnp.int16, (num_edges, LANES), 1)
-
-    def count_up(rows, row, low):
-        weights = wide[0:1, :]
-        up = lax.broadcasted_iota(i32, (rows, num_edges), 0)
-        picked = jnp.where(up == row, weights, 0.0)
-        parts = dot(jnp.concatenate(split3(picked), axis=0), low)
-        return parts[:rows] + parts[rows : 2 * rows] + parts[2 * rows :]
-
-    for k in range(wide_rows):
-        rows = slice(k * LANES, (k + 1) * LANES)
-        match = lax.broadcasted_iota(jnp.int16, (LANES, LANES), 1) == short(within_t[:, k : k + 1], (LANES, LANES))
-        flows[rows, :LANES] = one_hot(match)
-    degree_far = count_up(-(-peers // 16) * 16, rowf[4:5, :], flows[:, :LANES])
-    for q in range(peers):
-        degh[q] = jnp.broadcast_to(degree_far[q : q + 1, :], (8, LANES))
-
-    pl.semaphore_wait(barrier, peers + jnp.where(middle, 1, 0))
-
-    def degree_of(to):
-        return degh.at[to]
-
-    exchange(me, peers, degree_of, dback, deg_sem.at[0], deg_sem.at[1])
-    dback[me] = degh[me]
-
+
+    root_t = root.T
     for k in range(wide_rows):
         rows = slice(k * LANES, (k + 1) * LANES)
         flows[rows, :] = pair(-(root_t[:, k : k + 1] * sketch_ref[rows, :].astype(f32)))
 
-    list8[...] = jnp.full(list8.shape, -1, i32)
-    list8[:peers, :slot] = list_ref[...]
-    list_t = list8[...].T
-    for q in range(peers):
-        spread = jnp.broadcast_to(list_t[:, q : q + 1], (LANES, LANES))
-        list8b[q * LANES : (q + 1) * LANES, :] = spread.astype(jnp.int16)
-        list8row[0:1, q * LANES : (q + 1) * LANES] = list8[q : q + 1, :]
-        listb[q * slot : (q + 1) * slot, :] = spread[:slot]
-    for at in range(0, halo_len, LANES):
-        listrow[0:1, at : at + LANES] = listb[at : at + LANES, :].T[0:1, :]
-
-    ground_t = ground_ref[...].T
-    for j in range(high):
-        rows = slice(j * LANES, (j + 1) * LANES)
-        groundb[rows, :] = jnp.broadcast_to(ground_t[:, j : j + 1], (LANES, LANES))
-    for ref in (res, dirn, sol_ref, part):
-        ref[...] = jnp.zeros(ref.shape, f32)
+    def spread_columns():
+        for values, store in ((src_ref[...], srcb), (dst_ref[...], dstb), (held, wb)):
+            turned = values.T
+            for k in range(wide_rows):
+                rows = slice(k * LANES, (k + 1) * LANES)
+                store[rows, :] = jnp.broadcast_to(turned[:, k : k + 1], (LANES, LANES)).astype(store.dtype)
+        for ref in (res, dirn, sol_ref, part):
+            ref[...] = jnp.zeros(ref.shape, f32)
+
+    def count_up(rows, up_at, low, weights):
+        edges = weights.shape[1]
+        up = lax.broadcasted_iota(i32, (rows, edges), 0)
+        picked = jnp.where(up == up_at, weights, 0.0)
+        parts = dot_lanes(jnp.concatenate(split3(picked), axis=0), one_hot(down_rows(low, 0, LANES)))
+        return parts[:rows] + parts[rows : 2 * rows] + parts[2 * rows :]
+
+    def degree_of(to):
+        return degh.at[to]
+
+    def far_degree():
+        got = count_up(-(-peers // 16) * 16, rowf[2:3, :], rowf[3:4, :], wide[0:1, :num_edges])
+        for q in range(peers):
+            degh[q] = jnp.broadcast_to(got[q : q + 1, :], (8, LANES))
+        exchange(me, peers, degree_of, dback, deg_sem.at[0], deg_sem.at[1])
+        dback[me] = degh[me]
+
+    def spread_lists():
+        list8[...] = jnp.full(list8.shape, -1, i32)
+        list8[:peers, :slot] = list_ref[...]
+        list_t = list8[...].T
+        for q in range(peers):
+            list8row[0:1, q * LANES : (q + 1) * LANES] = list8[q : q + 1, :]
+            listb[q * slot : (q + 1) * slot, :] = jnp.broadcast_to(list_t[:, q : q + 1], (LANES, LANES))[:slot]
+        for at in range(0, halo_len, LANES):
+            listrow[0:1, at : at + LANES] = listb[at : at + LANES, :].T[0:1, :]
 
     def scatter_rows(at, rows):
         acc[:rows, :] = jnp.zeros((rows, 2 * columns), f32)
@@ -250,33 +240,52 @@
         hots = zip(along_lanes(srcb[rows, :], at, width), along_lanes(dstb[rows, :], at, width))
         return jnp.concatenate([signed(a, b) for a, b in hots], axis=1)
 
-    def gather_near(group, q):
+    def gather_near(group, q, tail=False):
         for off in range(0, quarter, etile):
             rows = pl.ds(pl.multiple_of(q * quarter + off, etile), etile)
             base = pl.multiple_of(group * GROUP, GROUP)
             hots = edge_hots(rows, base, GROUP)
-            part[rows, :] += halves(dot(hots, field[pl.ds(base, GROUP), :]))
+            got = part[rows, :] + halves(dot(hots, field[pl.ds(base, GROUP), :]))
+            part[rows, :] = got
+            if tail:
+                flows[rows, :] = pair(got * wb[rows, :])
 
     def own_degree():
-        low = one_hot(jnp.bitwise_and(srcb[...], jnp.int16(LANES - 1)) == lane_e)
         rows = -(-high // 16) * 16
-        got = count_up(rows, rowf[2:3, :], low)
-        low = one_hot(jnp.bitwise_and(dstb[...], jnp.int16(LANES - 1)) == lane_e)
-        got += count_up(rows, rowf[3:4, :], low)
-        up = lax.broadcasted_iota(i32, (rows, peers * LANES), 0)
+        got = jnp.zeros((rows, LANES), f32)
+        for row in (0, 1):
+            at = rowf[row : row + 1, :]
+            got += count_up(rows, at // LANES, at % LANES, wide[0:1, :num_edges])
         for q in range(peers):
-            wide[0:1, q * LANES : (q + 1) * LANES] = dback[q, 0:1, :]
-        picked = jnp.where(up == list8row[...] // LANES, wide[0:1, : peers * LANES], 0.0)
-        lane = lax.broadcasted_iota(jnp.int16, (peers * LANES, LANES), 1)
-        low = one_hot(jnp.bitwise_and(list8b[...], jnp.int16(LANES - 1)) == lane)
-        parts = dot(jnp.concatenate(split3(picked), axis=0), low)
-        got += parts[:rows] + parts[rows : 2 * rows] + parts[2 * rows :]
-        degown[...] = got[:high]
+            wide[1:2, q * LANES : (q + 1) * LANES] = dback[q, 0:1, :]
+        at = list8row[...]
+        landing = count_up(rows, jnp.where(at < 0, -1, at // LANES), at % LANES, wide[1:2, : peers * LANES])
+        degown[:high, :] = (got + landing)[:high]
+        degown[high:, :] = landing[:high]
 
     def degree_copy(kind, src, dst, target):
         return remote(src, dst, degline_sem.at[0, kind], degline_sem.at[1, kind], target)
 
     hpiece = even_piece(halo_len, 512)
+
+    def back_of(s):
+        def halo_of(to):
+            return yhalo.at[s, pl.ds(pl.multiple_of(to * slot, 8), slot)]
+
+        return me, peers, halo_of, back.at[s], back_sem.at[0, s], back_sem.at[1, s]
+
+    def send_back(s):
+        for at in range(0, halo_len, hpiece):
+            yhalo[s, at : at + hpiece, :] = scatter_rows(num_rows + at, hpiece)
+
+        if isinstance(s, int):
+            pl.semaphore_wait(barrier, peers + jnp.where(middle, 1, 0))
+        exchange(*back_of(s))
+        back[s, me] = yhalo[s, pl.ds(pl.multiple_of(me * slot, 8), slot), :]
+
+    send_back(0)
+    far_degree()
+    spread_lists()
 
     def stage(s, _):
         begin, last = s == 0, s == ITERS - 1
@@ -321,43 +330,35 @@
             total[s, rows, :] = mine[s, rows, :] + inner[s, rows, :]
             to_end(k).start()
 
-        for at in range(0, halo_len, hpiece):
-            yhalo[s, at : at + hpiece, :] = scatter_rows(num_rows + at, hpiece)
-
-        def halo_of(to):
-            return yhalo.at[s, pl.ds(pl.multiple_of(to * slot, 8), slot)]
-
-        back_args = (me, peers, halo_of, back.at[s], back_sem.at[0, s], back_sem.at[1, s])
-        exchange(*back_args)
-        back[s, me] = yhalo[s, pl.ds(pl.multiple_of(me * slot, 8), slot), :]
+        back_args = back_of(s)
 
         def group_rows(c, _):
             at = pl.multiple_of(c * GROUP, GROUP)
             local = scatter_rows(at, GROUP)
 
+            @pl.when(c == 0)
+            def _():
+                exchange_wait(*back_args)
+                retb[...] = pair(back[s].reshape(halo_len, columns))
+
+            pick = one_hot(down_rows(listrow[...], at, GROUP))
+            own[s, pl.ds(at, GROUP), :] = local + halves(dot(pick, retb[...]))
+
+            @pl.when(at_end)
+            def _():
+                for j in range(per):
+                    to_middle(c * per + j).start()
+
             @pl.when(jnp.logical_and(begin, c == 0))
             def _():
                 exchange_wait(me, peers, degree_of, dback, deg_sem.at[0], deg_sem.at[1])
                 own_degree()
 
-            @pl.when(c == 0)
-            def _():
-                exchange_wait(*back_args)
-                retb[...] = pair(back[s].reshape(halo_len, columns))
-
-            @pl.when(jnp.logical_and(begin, c == 0))
-            def _():
                 @pl.when(at_end)
                 def _():
                     degree_copy(0, degown, degouter, near).start()
 
-            pick = one_hot(down_rows(listrow[...], at, GROUP))
-            own[s, pl.ds(at, GROUP), :] = local + halves(dot(pick, retb[...]))
-
-            @pl.when(at_end)
-            def _():
-                for j in range(per):
-                    to_middle(c * per + j).start()
+                spread_columns()
 
             @pl.when(jnp.logical_and(middle, c == groups - 2))
             def _():
@@ -386,10 +387,12 @@
             def _():
                 degree_copy(2, degtotal, degtotal, near).wait_recv()
 
-            inverse_t = (1.0 / (degtotal[...] + ground_ref[...])).T
+            inverse_t = (1.0 / (degtotal[:high, :] + ground_ref[...])).T
+            held_t = (degtotal[high:, :] + ground_ref[...]).T
             for j in range(high):
                 rows = slice(j * LANES, (j + 1) * LANES)
                 invb[rows, :] = jnp.broadcast_to(inverse_t[:, j : j + 1], (LANES, LANES))
+                groundb[rows, :] = jnp.broadcast_to(held_t[:, j : j + 1], (LANES, LANES))
 
         def step(k, _):
             rows = piece_rows(k)
@@ -441,10 +444,15 @@
         landed[s, me] = listed[s, pl.ds(pl.multiple_of(me * slot, 8), slot), :]
 
         def near_tail(q, _):
-            gather_near(groups - 1, q)
+            gather_near(groups - 1, q, True)
             return 0
 
         lax.fori_loop(0, 4, near_tail, 0)
+
+        @pl.when(jnp.logical_not(last))
+        def _():
+            send_back(s + 1)
+
         exchange_wait(*land_args)
         field[num_rows:, :] = pair(landed[s].reshape(halo_len, columns))
 
@@ -516,7 +524,7 @@
     flat_halo = vmem((ITERS, halo_len, columns), f32)
     rows_f32 = vmem((num_rows, columns), f32)
     line = vmem((ITERS, num_rows, columns), f32)
-    small = vmem((high, LANES), f32)
+    small = vmem((2 * high, LANES), f32)
     spread = vmem((num_edges, LANES), i16)
     scratch = [
         vmem((8, num_edges), i32), spread, spread,
@@ -528,7 +536,7 @@
         vmem((num_edges, 2 * columns), bf16), line, line, line, line, line,
         flat_halo, halo, flat_halo, halo,
         vmem((wide_rows, LANES), f32), vmem((peers8, LANES), i32),
-        vmem((peers * LANES, LANES), i16), vmem((1, peers * LANES), i32),
+        vmem((1, peers * LANES), i32),
         small, small, small, small, small, vmem((peers, 8, LANES), f32), vmem((peers, 8, LANES), f32),
         dma((2, ITERS, peers)), dma((2, ITERS, peers)), dma((2, peers)), dma((2, ITERS, 3, count)), dma((2, 3)),
     ]

time: 155 us -> 146 us (0.942)
  Pallas kernels: 151 us -> 141 us
    pallas_call x1, Pallas kernels: 151 us -> 141 us  [local(): pl.pallas_call(functools.partial(kernel, peers), in_specs=[in_vmem] * 6 +...]
where the time goes in v2:
time: 146 us
  Pallas kernels  141 us (97%)
  local copies, waits for them, and re-layouts  2.88 us (2%)
    pallas_call x1, Pallas kernels, local(): pl.pallas_call(functools.partial(kernel, peers), in_specs=[in_vmem] * 6 +...  141 us

profile of v2, /device:TPU:0, one launch (start us, length us, event | category | flops | bytes accessed | tf_op | source)
XLA Modules:
  0.0 145.6 jit_solution(9261414706378573740)
XLA Ops:
  1.3 141.4 %sketch.1 = (f32[2048,128]{1,0:T(8,128)}, f32[32,128]{1,0:T(8,128)}) custom-call(bf16[4096,128]{1,0:T(8,128)(2,1)} %sketch_ref.1, f32[32,128]{1,0:T(8,128)} %bitcast.6, f32[16,128]{1,0:T(8,128)} %bitcast.10, s32[32,128]{1,0:T(8,128)} %bitcast.7, s32[32,128]{1,0:T(8,128)} %bitcast.8, s32[8,48]{1,0:T(8,128)} %bitcast.11, s32[1]{0:T(128)S(6)} %copy.11.count_ref), custom_call_target="tpu_custom_call" | custom-call | tf_op jit(solution)/shard_map/sketch/pallas_call | solution.py:544
  142.7 0.0 copy-start
  142.7 2.3 %copy.12 = f32[2048,128]{1,0:T(8,128)} copy(f32[2048,128]{1,0:T(8,128)} %get-tuple-element.8) | data formatting | bytes 2097152
  145.0 0.0 copy-done
  145.0 0.6 copy.13
Async XLA Ops:
  142.7 2.3 %copy-start = (f32[32,128]{1,0:T(8,128)S(1)}, f32[32,128]{1,0:T(8,128)}, u32[]{:S(2)}) copy-start(f32[32,128]{1,0:T(8,128)} %get-tuple-element.5) | copy-start | bytes 49156

commit v3 on v2

v3 whole, which is shorter than its diff:
```python
import functools

import jax
import jax.numpy as jnp
from jax import lax
from jax.experimental import pallas as pl
from jax.experimental.pallas import tpu as pltpu
from jax.sharding import PartitionSpec as P

ITERS = 3

lam_low = 0.05
lam_high = 2.0
LANES = 128
VMEM_LIMIT = 62 * 1024 * 1024
GROUP = 512
PIECE = 128
LAG = 4
LEAD = 2


def chebyshev_terms(steps):
    centre = (lam_high + lam_low) / 2.0
    half_width = (lam_high - lam_low) / 2.0
    sigma_val = centre / half_width
    rho_prev = 1.0 / sigma_val
    pairs = []
    for count_idx in range(steps - 1):
        rho_next = 1.0 / (2.0 * sigma_val - rho_prev)
        pairs.append((rho_next * rho_prev, 2.0 * rho_next / half_width))
        rho_prev = rho_next
    return (1.0 / centre, pairs)


def split2(x):
    hi = x.astype(jnp.bfloat16)
    lo = (x - hi.astype(jnp.float32)).astype(jnp.bfloat16)
    return hi, lo


def split3(x):
    hi = x.astype(jnp.bfloat16)
    rest = x - hi.astype(jnp.float32)
    mid, lo = split2(rest)
    return hi, mid, lo


def pair(x):
    return jnp.concatenate(split2(x), axis=1)


def halves(x):
    n = x.shape[1] // 2
    return x[:, :n] + x[:, n:]


def dot(a, b):
    return jnp.dot(a, b, preferred_element_type=jnp.float32)


def dot_lanes(a, b):
    return lax.dot_general(a, b, (((1,), (1,)), ((), ())), preferred_element_type=jnp.float32)


def signed(is_src, is_dst):
    one, none = jnp.ones(is_src.shape, jnp.bfloat16), jnp.zeros(is_src.shape, jnp.bfloat16)
    return jnp.where(is_src, one, jnp.where(is_dst, -one, none))


def one_hot(match):
    return jnp.where(match, jnp.ones(match.shape, jnp.bfloat16), jnp.zeros(match.shape, jnp.bfloat16))


def short(x, shape):
    return jnp.broadcast_to(jnp.asarray(x, jnp.int32), shape).astype(jnp.int16)


def down_rows(row, at, rows):
    shape = (rows, row.shape[1])
    return lax.broadcasted_iota(jnp.int16, shape, 0) == jnp.broadcast_to((row - at).astype(jnp.int16), shape)


def along_lanes(spread, at, width):
    parts = []
    lane = lax.broadcasted_iota(jnp.int16, spread.shape, 1)
    for off in range(0, width, LANES):
        parts.append(lane + short(at + off, spread.shape) == spread)
    return parts


def even_piece(total, most):
    return max(n for n in range(8, most + 1, 8) if total % n == 0)


def remote(src, dst, send_sem, recv_sem, target):
    return pltpu.make_async_remote_copy(
        src_ref=src, dst_ref=dst, send_sem=send_sem, recv_sem=recv_sem,
        device_id=target, device_id_type=pl.DeviceIdType.MESH,
    )


def exchange(place, src, dst, send_sem, recv_sem):
    me, peers, target = place

    def start(off, _):
        to = lax.rem(me + off, peers)
        remote(src(to), dst.at[me], send_sem.at[off], recv_sem.at[off], target(to)).start()
        return 0

    lax.fori_loop(1, peers, start, 0)


def exchange_wait(place, src, dst, send_sem, recv_sem):
    me, peers, target = place

    def wait(off, _):
        to = lax.rem(me + off, peers)
        origin = lax.rem(me + peers - off, peers)
        remote(src(to), dst.at[origin], send_sem.at[off], recv_sem.at[off], target(to)).wait()
        return 0

    lax.fori_loop(1, peers, wait, 0)


def kernel(
    peers, sketch_ref, weight_ref, ground_ref, src_ref, dst_ref, list_ref, count_ref, out_ref, gap_ref,
    rowf, srcb, dstb, wide, wb, listb, listrow, groundb, invb, res, dirn, sol, field, part, acc, retb,
    flows, own, outer, inner, mine, total, yhalo, back, listed, landed, mask, list8, list8row,
    degown, degouter, deginner, degmine, degtotal, degh, dback,
    new_src, new_dst, held, new_held, new_list, new_ground, gaps, gaps_in, sol_in,
    back_sem, land_sem, deg_sem, line_sem, degline_sem, swap_sem, sol_sem,
):
    first, pairs = chebyshev_terms(ITERS)
    me, z = lax.axis_index("vtx"), lax.axis_index("edg")
    slot, columns = back.shape[2], back.shape[3]
    halo_len = peers * slot
    wide_rows = src_ref.shape[0]
    num_edges = wide_rows * LANES
    num_rows = out_ref.shape[0]
    high = num_rows // LANES
    ktile = min(1024, num_edges)
    etile = 1024
    quarter = num_edges // 4
    groups = num_rows // GROUP
    per = GROUP // PIECE
    count = num_rows // PIECE
    core, half = lax.rem(me, 2), z // 2

    def mirrored(at):
        return at + core * (3 - 2 * at)

    u = mirrored(z)
    moves = u >= 2
    stays = u < 2
    block = 2 * (me // 2) + half
    other_core = {"vtx": me + 1 - 2 * core}
    across = {"edg": z + 1 - 2 * lax.rem(z, 2)}
    swap_with = {"vtx": me + 1 - 2 * core, "edg": z + 2 - 4 * half}
    inward = {"edg": mirrored(jnp.where(u == 0, 1, u - 1))}
    totals_to = [other_core, {"edg": mirrored(0)}, {"vtx": me + 1 - 2 * core, "edg": mirrored(0)}]
    outward = {"edg": mirrored(jnp.where(u == 1, 2, 3))}

    def home(to):
        return {"vtx": to}

    def hosted(to):
        return {"vtx": 2 * (to // 2) + core, "edg": 2 * lax.rem(to, 2) + lax.rem(z, 2)}

    at_home, at_host = (me, peers, home), (block, peers, hosted)
    f32, bf16, i32 = jnp.float32, jnp.bfloat16, jnp.int32

    barrier = pltpu.get_barrier_semaphore()

    def greet(target):
        pl.semaphore_signal(barrier, inc=1, device_id=target, device_id_type=pl.DeviceIdType.MESH)

    def greet_peer(off, _):
        greet({"vtx": lax.rem(me + off, peers)})
        return 0

    lax.fori_loop(1, peers, greet_peer, 0)

    def greet_far(q, _):
        greet({"vtx": 2 * q + core, "edg": z + 2 - 4 * half})
        return 0

    lax.fori_loop(0, peers // 2, greet_far, 0)

    @pl.when(z > 0)
    def _():
        greet({"edg": z - 1})

    @pl.when(z < 3)
    def _():
        greet({"edg": z + 1})

    @pl.when(lax.rem(u, 2) == 1)
    def _():
        greet({"vtx": me + 1 - 2 * core, "edg": mirrored(u - 1)})

    @pl.when(moves)
    def _():
        greet(swap_with)

    greeted = peers - 1 + peers // 2 + lax.rem(u, 2) + jnp.where(moves, 1, 0)
    greeted += jnp.where(z > 0, 1, 0) + jnp.where(z < 3, 1, 0)

    shape = (wide_rows, LANES)
    position = lax.broadcasted_iota(i32, shape, 0) * LANES + lax.broadcasted_iota(i32, shape, 1)
    live = position < count_ref[0]
    src, dst = src_ref[...], dst_ref[...]
    slots = dst - num_rows
    weight = jnp.where(live, weight_ref[...], 0.0)
    apart = jnp.logical_and(live, src != dst)
    held[...] = jnp.where(apart, weight_ref[...], 0.0)
    root = jnp.sqrt(held[...])
    list8[...] = jnp.full(list8.shape, -1, i32)
    list8[:peers, :slot] = list_ref[...]

    def swaps():
        pairs_of = [(src_ref, new_src), (dst_ref, new_dst), (held, new_held), (list8, new_list), (ground_ref, new_ground)]
        return [remote(a, b, swap_sem.at[0, i], swap_sem.at[1, i], swap_with) for i, (a, b) in enumerate(pairs_of)]

    @pl.when(stays)
    def _():
        new_src[...] = src_ref[...]
        new_dst[...] = dst_ref[...]
        new_held[...] = held[...]
        new_list[...] = list8[...]
        new_ground[...] = ground_ref[...]

    mask[...] = jnp.where(apart, 1.0, 0.0)
    peer_of = jnp.where(slots < 0, -1, slots // slot)
    within = jnp.where(slots < 0, -1, slots % slot)
    for k in range(wide_rows):
        cols = slice(k * LANES, (k + 1) * LANES)
        rowf[0:1, cols] = src[k : k + 1, :]
        rowf[1:2, cols] = dst[k : k + 1, :]
        rowf[2:3, cols] = peer_of[k : k + 1, :]
        rowf[3:4, cols] = within[k : k + 1, :]
        wide[0:1, cols] = weight[k : k + 1, :]

    root_t = root.T
    for k in range(wide_rows):
        rows = slice(k * LANES, (k + 1) * LANES)
        flows[rows, :] = pair(-(root_t[:, k : k + 1] * sketch_ref[rows, :].astype(f32)))

    def spread_columns():
        for values, store in ((new_src, srcb), (new_dst, dstb), (new_held, wb)):
            turned = values[...].T
            for k in range(wide_rows):
                rows = slice(k * LANES, (k + 1) * LANES)
                store[rows, :] = jnp.broadcast_to(turned[:, k : k + 1], (LANES, LANES)).astype(store.dtype)
        for k in range(wide_rows):
            cols = slice(k * LANES, (k + 1) * LANES)
            rowf[4:5, cols] = new_src[k : k + 1, :]
            rowf[5:6, cols] = new_dst[k : k + 1, :]
        spread_lists(new_list, 1)
        for ref in (res, dirn, sol, part):
            ref[...] = jnp.zeros(ref.shape, f32)

    def count_up(rows, up_at, low, weights):
        edges = weights.shape[1]
        up = lax.broadcasted_iota(i32, (rows, edges), 0)
        picked = jnp.where(up == up_at, weights, 0.0)
        parts = dot_lanes(jnp.concatenate(split3(picked), axis=0), one_hot(down_rows(low, 0, LANES)))
        return parts[:rows] + parts[rows : 2 * rows] + parts[2 * rows :]

    def degree_of(to):
        return degh.at[to]

    def far_degree():
        got = count_up(-(-peers // 16) * 16, rowf[2:3, :], rowf[3:4, :], wide[0:1, :num_edges])
        for q in range(peers):
            degh[q] = jnp.broadcast_to(got[q : q + 1, :], (8, LANES))
        exchange(at_home, degree_of, dback, deg_sem.at[0], deg_sem.at[1])
        dback[me] = degh[me]

    def spread_lists(lists, row):
        list_t = lists[...].T
        for q in range(peers):
            listb[q * slot : (q + 1) * slot, :] = jnp.broadcast_to(list_t[:, q : q + 1], (LANES, LANES))[:slot]
        for at in range(0, halo_len, LANES):
            listrow[row : row + 1, at : at + LANES] = listb[at : at + LANES, :].T[0:1, :]

    def scatter_rows(at, rows, edges):
        acc[:rows, :] = jnp.zeros((rows, 2 * columns), f32)

        def body(k, _):
            cols = pl.ds(pl.multiple_of(k * ktile, ktile), ktile)
            pick = signed(down_rows(rowf[edges : edges + 1, cols], at, rows), down_rows(rowf[edges + 1 : edges + 2, cols], at, rows))
            acc[:rows, :] += dot(pick, flows[cols, :])
            return 0

        lax.fori_loop(0, num_edges // ktile, body, 0)
        return halves(acc[:rows, :])

    def edge_hots(rows, at, width):
        hots = zip(along_lanes(srcb[rows, :], at, width), along_lanes(dstb[rows, :], at, width))
        return jnp.concatenate([signed(a, b) for a, b in hots], axis=1)

    def gather_near(group, q, tail=False):
        for off in range(0, quarter, etile):
            rows = pl.ds(pl.multiple_of(q * quarter + off, etile), etile)
            base = pl.multiple_of(group * GROUP, GROUP)
            hots = edge_hots(rows, base, GROUP)
            got = part[rows, :] + halves(dot(hots, field[pl.ds(base, GROUP), :]))
            part[rows, :] = got
            if tail:
                flows[rows, :] = pair(got * wb[rows, :])

    def own_degree():
        rows = -(-high // 16) * 16
        got = jnp.zeros((rows, LANES), f32)
        for row in (0, 1):
            at = rowf[row : row + 1, :]
            got += count_up(rows, at // LANES, at % LANES, wide[0:1, :num_edges])
        for q in range(peers):
            list8row[0:1, q * LANES : (q + 1) * LANES] = list8[q : q + 1, :]
            wide[1:2, q * LANES : (q + 1) * LANES] = dback[q, 0:1, :]
        at = list8row[...]
        landing = count_up(rows, jnp.where(at < 0, -1, at // LANES), at % LANES, wide[1:2, : peers * LANES])
        degown[:high, :] = (got + landing)[:high]
        degown[high:, :] = landing[:high]

    def degree_copy(kind, land, src, dst, target):
        return remote(src, dst, degline_sem.at[0, kind], degline_sem.at[1, land], target)

    def degree_sum():
        return degree_copy(0, 0, degown, degouter, inward)

    def degree_part():
        return degree_copy(1, 1, degmine, deginner, inward)

    def degree_total(j):
        return degree_copy(2 + j, 2, degtotal, degtotal, totals_to[j])

    hpiece = even_piece(halo_len, 512)

    def back_of(s, place):
        def halo_of(to):
            return yhalo.at[s, pl.ds(pl.multiple_of(to * slot, 8), slot)]

        return place, halo_of, back.at[s], back_sem.at[0, s], back_sem.at[1, s]

    def send_back(s, place, edges):
        for at in range(0, halo_len, hpiece):
            yhalo[s, at : at + hpiece, :] = scatter_rows(num_rows + at, hpiece, edges)
        if edges == 0:
            pl.semaphore_wait(barrier, greeted)
        exchange(*back_of(s, place))
        back[s, place[0]] = yhalo[s, pl.ds(pl.multiple_of(place[0] * slot, 8), slot), :]

    send_back(0, at_home, 0)

    @pl.when(moves)
    def _():
        for copy in swaps():
            copy.start()

    far_degree()
    spread_lists(list8, 0)

    def piece_rows(k):
        return pl.ds(pl.multiple_of(k * PIECE, PIECE), PIECE)

    def line_copy(s, kind, land, k, src, dst, target):
        rows = piece_rows(k)
        return remote(
            src.at[s, rows], dst.at[s, rows], line_sem.at[0, s, kind, k], line_sem.at[1, s, land, k], target
        )

    def own_rows(s, c, place, edges):
        at = pl.multiple_of(c * GROUP, GROUP)
        local = scatter_rows(at, GROUP, edges)

        @pl.when(c == 0)
        def _():
            exchange_wait(*back_of(s, place))
            retb[...] = pair(back[s].reshape(halo_len, columns))

        pick = one_hot(down_rows(listrow[min(edges, 1) : min(edges, 1) + 1, :], at, GROUP))
        own[s, pl.ds(at, GROUP), :] = local + halves(dot(pick, retb[...]))

    def update(s, rows, keep, push, last):
        old = dirn[rows, :]
        residual = res[rows, :] - (groundb[rows, :] * old + total[s, rows, :])
        direction = keep * old + push * invb[rows, :] * residual
        shown = sol[rows, :] + direction
        res[rows, :] = residual
        dirn[rows, :] = direction
        sol[rows, :] = shown
        field[rows, :] = pair(jnp.where(last, shown, direction))

    def pick_group(s, group):
        base = pl.multiple_of(group * GROUP, GROUP)
        for at in range(0, halo_len, hpiece):
            spread = listb[at : at + hpiece, :].astype(jnp.int16)
            hots = jnp.concatenate([one_hot(m) for m in along_lanes(spread, base, GROUP)], axis=1)
            got = halves(dot(hots, field[pl.ds(base, GROUP), :]))
            listed[s, at : at + hpiece, :] = jnp.where(group == 0, got, listed[s, at : at + hpiece, :] + got)

    def sum_at_home(keep, push, last):
        def to_inward(k):
            return line_copy(0, 0, 0, k, own, outer, inward)

        def part_inward(k):
            return line_copy(0, 1, 1, k, mine, inner, inward)

        def give_total(k, j):
            return line_copy(0, 2 + j, 2, k, total, total, totals_to[j])

        def pass_partial(k):
            rows = piece_rows(k)
            to_inward(k).wait_recv()
            mine[0, rows, :] = own[0, rows, :] + outer[0, rows, :]
            part_inward(k).start()

        sends = jnp.logical_or(u == 0, u == 3)

        def group_rows(c, _):
            own_rows(0, c, at_home, 0)

            @pl.when(sends)
            def _():
                for j in range(per):
                    to_inward(c * per + j).start()

            @pl.when(c == 0)
            def _():
                exchange_wait(at_home, degree_of, dback, deg_sem.at[0], deg_sem.at[1])
                own_degree()

                @pl.when(sends)
                def _():
                    degree_sum().start()

                @pl.when(moves)
                def _():
                    for copy in swaps():
                        copy.wait()

                spread_columns()

            @pl.when(jnp.logical_and(u == 2, c == groups - 2))
            def _():
                degree_sum().wait_recv()
                degmine[...] = degown[...] + degouter[...]
                degree_part().start()
                for k in range(LAG):
                    pass_partial(k)

            return 0

        lax.fori_loop(0, groups, group_rows, 0)

        @pl.when(u == 1)
        def _():
            degree_sum().wait_recv()
            degree_part().wait_recv()
            degtotal[...] = (degown[...] + degouter[...]) + deginner[...]
            for j in range(3):
                degree_total(j).start()

        @pl.when(u != 1)
        def _():
            degree_total(0).wait_recv()

        inverse_t = (1.0 / (degtotal[:high, :] + new_ground[...])).T
        held_t = (degtotal[high:, :] + new_ground[...]).T
        for j in range(high):
            rows = slice(j * LANES, (j + 1) * LANES)
            invb[rows, :] = jnp.broadcast_to(inverse_t[:, j : j + 1], (LANES, LANES))
            groundb[rows, :] = jnp.broadcast_to(held_t[:, j : j + 1], (LANES, LANES))

        def step(k, _):
            rows = piece_rows(k)

            @pl.when(jnp.logical_and(u == 2, k + LAG < count))
            def _():
                pass_partial(k + LAG)

            @pl.when(u == 1)
            def _():
                to_inward(k).wait_recv()
                part_inward(k).wait_recv()
                total[0, rows, :] = (own[0, rows, :] + outer[0, rows, :]) + inner[0, rows, :]
                for j in range(3):
                    give_total(k, j).start()

            @pl.when(u != 1)
            def _():
                give_total(k, 0).wait_recv()

            update(0, rows, keep, push, last)
            group, j = k // per, lax.rem(k, per)

            @pl.when(j == per - 1)
            def _():
                pick_group(0, group)

            @pl.when(group > 0)
            def _():
                gather_near(group - 1, j)

            return 0

        lax.fori_loop(0, count, step, 0)

        def line_done(k, _):
            @pl.when(sends)
            def _():
                to_inward(k).wait_send()

            @pl.when(u == 2)
            def _():
                part_inward(k).wait_send()

            @pl.when(u == 1)
            def _():
                for j in range(3):
                    give_total(k, j).wait_send()

            return 0

        lax.fori_loop(0, count, line_done, 0)

        @pl.when(sends)
        def _():
            degree_sum().wait_send()

        @pl.when(u == 2)
        def _():
            degree_part().wait_send()

        @pl.when(u == 1)
        def _():
            for j in range(3):
                degree_total(j).wait_send()

    def show(m, held_in):
        rows = pl.ds(pl.multiple_of(m * 2 * PIECE, 2 * PIECE), 2 * PIECE)
        return remote(held_in.at[rows], sol_in.at[rows], sol_sem.at[0, m], sol_sem.at[1, m], outward)

    def first_show(m):
        return show(m, sol)

    def next_show(m):
        return show(m, sol_in)

    def forward(m):
        first_show(m).wait_recv()
        next_show(m).start()

    def sum_at_host(s, keep, push, last):
        def lend(k):
            return line_copy(s, 0, 0, k, own, outer, other_core)

        def cross(k):
            return line_copy(s, 1, 1, k, mine, inner, across)

        def share(k):
            return line_copy(s, 2, 2, k, total, total, other_core)

        def pair_sum(c):
            for j in range(per // 2):
                k = c * per + 2 * j + core
                rows = piece_rows(k)
                lend(k).wait_recv()
                mine[s, rows, :] = own[s, rows, :] + outer[s, rows, :]
                cross(k).start()

        def group_rows(c, _):
            own_rows(s, c, at_host, 4)
            for j in range(per // 2):
                lend(c * per + 2 * j + 1 - core).start()

            @pl.when(c > 0)
            def _():
                pair_sum(c - 1)

            return 0

        lax.fori_loop(0, groups, group_rows, 0)
        pair_sum(groups - 1)

        def step(m, _):
            k = 2 * m + core
            rows = piece_rows(k)
            cross(k).wait_recv()
            total[s, rows, :] = mine[s, rows, :] + inner[s, rows, :]
            share(k).start()
            share(2 * m + 1 - core).wait_recv()
            update(s, pl.ds(pl.multiple_of(m * 2 * PIECE, 2 * PIECE), 2 * PIECE), keep, push, last)

            @pl.when(jnp.logical_and(last, u == 1))
            def _():
                first_show(m).start()

            @pl.when(jnp.logical_and(jnp.logical_and(last, u == 2), m >= LEAD))
            def _():
                forward(m - LEAD)

            group, j = m // (per // 2), lax.rem(m, per // 2)

            @pl.when(j == per // 2 - 1)
            def _():
                pick_group(s, group)

            @pl.when(group > 0)
            def _():
                gather_near(group - 1, 2 * j)
                gather_near(group - 1, 2 * j + 1)

            return 0

        lax.fori_loop(0, count // 2, step, 0)

        def sent(m, _):
            lend(2 * m + 1 - core).wait_send()
            cross(2 * m + core).wait_send()
            share(2 * m + core).wait_send()
            return 0

        lax.fori_loop(0, count // 2, sent, 0)

    def stage(s, _):
        begin, last = s == 0, s == ITERS - 1
        keep, push = jnp.float32(0.0), jnp.float32(first)
        for at, (k_coef, p_coef) in enumerate(pairs):
            keep = jnp.where(s == at + 1, jnp.float32(k_coef), keep)
            push = jnp.where(s == at + 1, jnp.float32(p_coef), push)

        @pl.when(begin)
        def _():
            sum_at_home(keep, push, last)

        @pl.when(jnp.logical_not(begin))
        def _():
            sum_at_host(s, keep, push, last)

        def listed_of(to):
            return listed.at[s, pl.ds(pl.multiple_of(to * slot, 8), slot)]

        land_args = (at_host, listed_of, landed.at[s], land_sem.at[0, s], land_sem.at[1, s])
        exchange(*land_args)
        landed[s, block] = listed[s, pl.ds(pl.multiple_of(block * slot, 8), slot), :]

        def near_tail(q, _):
            gather_near(groups - 1, q, True)
            return 0

        lax.fori_loop(0, 4, near_tail, 0)

        @pl.when(jnp.logical_not(last))
        def _():
            send_back(s + 1, at_host, 4)

        @pl.when(jnp.logical_and(last, u == 2))
        def _():
            for m in range(count // 2 - LEAD, count // 2):
                forward(m)

        exchange_wait(*land_args)
        field[num_rows:, :] = pair(landed[s].reshape(halo_len, columns))

        def gather_far(k):
            rows = pl.ds(pl.multiple_of(k * etile, etile), etile)
            gap = part[rows, :] + halves(dot(edge_hots(rows, num_rows, halo_len), field[num_rows:, :]))
            part[rows, :] = jnp.zeros(gap.shape, f32)
            return rows, gap

        @pl.when(jnp.logical_not(last))
        def _():
            def make_flows(k, _):
                rows, gap = gather_far(k)
                flows[rows, :] = pair(gap * wb[rows, :])
                return 0

            lax.fori_loop(0, num_edges // etile, make_flows, 0)

        @pl.when(last)
        def _():
            def make_gaps(k, _):
                rows, gap = gather_far(k)
                square = gap * gap
                for i in range(etile // LANES):
                    turned = square[i * LANES : (i + 1) * LANES, :].T
                    row = pl.ds(k * (etile // LANES) + i, 1)
                    gaps[row, :] = jnp.sum(turned, axis=0, keepdims=True)
                return 0

            lax.fori_loop(0, num_edges // etile, make_gaps, 0)

        return 0

    lax.fori_loop(0, ITERS, stage, 0)

    def gaps_home():
        return remote(gaps, gaps_in, swap_sem.at[0, 5], swap_sem.at[1, 5], swap_with)

    @pl.when(stays)
    def _():
        out_ref[...] = sol[...]
        gap_ref[...] = mask[...] * gaps[...] / columns

    @pl.when(moves)
    def _():
        gaps_home().start()

    @pl.when(u == 3)
    def _():
        for m in range(count // 2):
            first_show(m).wait_recv()

    @pl.when(jnp.logical_or(u == 1, u == 2))
    def _():
        for m in range(count // 2):
            first_show(m).wait_send()

    @pl.when(moves)
    def _():
        out_ref[...] = sol_in[...]
        gaps_home().wait()
        gap_ref[...] = mask[...] * gaps_in[...] / columns


def local(sketch_cols, edge_weight, ground, src_local, dst_index, send_rows, edge_count):
    peers = lax.axis_size("vtx")
    num_rows, num_edges = ground.shape[0], edge_weight.shape[0]
    slot, columns = send_rows.shape[2], sketch_cols.shape[1]
    halo_len, high, wide_rows = peers * slot, num_rows // LANES, num_edges // LANES
    count = num_rows // PIECE
    f32, bf16, i32, i16 = jnp.float32, jnp.bfloat16, jnp.int32, jnp.int16
    vmem, dma = pltpu.VMEM, pltpu.SemaphoreType.DMA
    peers8 = -(-peers // 8) * 8
    halo = vmem((ITERS, peers, slot, columns), f32)
    flat_halo = vmem((ITERS, halo_len, columns), f32)
    rows_f32 = vmem((num_rows, columns), f32)
    line = vmem((ITERS, num_rows, columns), f32)
    small = vmem((2 * high, LANES), f32)
    spread = vmem((num_edges, LANES), i16)
    wide_f32 = vmem((wide_rows, LANES), f32)
    scratch = [
        vmem((8, num_edges), i32), spread, spread,
        vmem((8, max(num_edges, peers * LANES)), f32), vmem((num_edges, LANES), f32),
        vmem((halo_len, LANES), i32), vmem((2, halo_len), i32),
        rows_f32, rows_f32, rows_f32, rows_f32, rows_f32,
        vmem((num_rows + halo_len, 2 * columns), bf16), vmem((num_edges, columns), f32),
        vmem((GROUP, 2 * columns), f32), vmem((halo_len, 2 * columns), bf16),
        vmem((num_edges, 2 * columns), bf16), line, line, line, line, line,
        flat_halo, halo, flat_halo, halo,
        vmem((wide_rows, LANES), f32), vmem((peers8, LANES), i32),
        vmem((1, peers * LANES), i32),
        small, small, small, small, small, vmem((peers, 8, LANES), f32), vmem((peers, 8, LANES), f32),
        vmem((wide_rows, LANES), i32), vmem((wide_rows, LANES), i32), wide_f32, wide_f32,
        vmem((peers8, LANES), i32), vmem((high, LANES), f32), wide_f32, wide_f32, rows_f32,
        dma((2, ITERS, peers)), dma((2, ITERS, peers)), dma((2, peers)), dma((2, ITERS, 5, count)), dma((2, 5)),
        dma((2, 6)), dma((2, count // 2)),
    ]
    in_vmem = pl.BlockSpec(memory_space=pltpu.VMEM)
    solution, gaps = pl.pallas_call(
        functools.partial(kernel, peers),
        in_specs=[in_vmem] * 6 + [pl.BlockSpec(memory_space=pltpu.SMEM)],
        out_specs=[in_vmem] * 2,
        out_shape=[jax.ShapeDtypeStruct((num_rows, columns), f32), jax.ShapeDtypeStruct((wide_rows, LANES), f32)],
        scratch_shapes=scratch,
        compiler_params=pltpu.CompilerParams(collective_id=0, has_side_effects=True, vmem_limit_bytes=VMEM_LIMIT),
        name="sketch",
    )(
        sketch_cols, edge_weight.reshape(wide_rows, LANES), ground.reshape(high, LANES),
        src_local.reshape(wide_rows, LANES), dst_index.reshape(wide_rows, LANES), send_rows[0], edge_count,
    )
    return solution, gaps.reshape(-1)


def solution(mesh):
    in_specs = (
        P(("vtx", "edg"), None),
        P(("vtx", "edg")),
        P("vtx"),
        P(("vtx", "edg")),
        P(("vtx", "edg")),
        P(("vtx", "edg"), None, None),
        P(("vtx", "edg")),
    )
    out_specs = (P("vtx", None), P(("vtx", "edg")))
    return jax.shard_map(local, mesh=mesh, in_specs=in_specs, out_specs=out_specs, check_vma=False)
```

time: 146 us -> 139 us (0.952)
  the two profiles are of different devices: /device:TPU:0 before, /device:TPU:9 now
where the time goes in v3:
time: 139 us; the launch traced here: 138 us
  Pallas kernels  134 us (96%)
  local copies, waits for them, and re-layouts  2.88 us (2%)
    pallas_call x1, Pallas kernels, local(): pl.pallas_call(functools.partial(kernel, peers), in_specs=[in_vmem] * 6 +...  134 us
    unnamed x4, local copies, waits for them, and re-layouts  2.88 us

profile of v3, /device:TPU:9, one launch (start us, length us, event | category | flops | bytes accessed | tf_op | source)
XLA Modules:
  0.0 138.5 jit_solution(3536034771126299382)
XLA Ops:
  1.3 134.3 %sketch.1 = (f32[2048,128]{1,0:T(8,128)}, f32[32,128]{1,0:T(8,128)}) custom-call(bf16[4096,128]{1,0:T(8,128)(2,1)} %sketch_ref.1, f32[32,128]{1,0:T(8,128)} %bitcast.6, f32[16,128]{1,0:T(8,128)} %bitcast.10, s32[32,128]{1,0:T(8,128)} %bitcast.7, s32[32,128]{1,0:T(8,128)} %bitcast.8, s32[8,48]{1,0:T(8,128)} %bitcast.11, s32[1]{0:T(128)S(6)} %copy.11.count_ref), custom_call_target="tpu_custom_call" | custom-call | tf_op jit(solution)/shard_map/sketch/pallas_call | solution.py:762
  135.6 0.0 copy-start
  135.6 2.3 %copy.12 = f32[2048,128]{1,0:T(8,128)} copy(f32[2048,128]{1,0:T(8,128)} %get-tuple-element.8) | data formatting | bytes 2097152
  137.8 0.0 copy-done
  137.8 0.6 copy.13
Async XLA Ops:
  135.6 2.3 %copy-start = (f32[32,128]{1,0:T(8,128)S(1)}, f32[32,128]{1,0:T(8,128)}, u32[]{:S(2)}) copy-start(f32[32,128]{1,0:T(8,128)} %get-tuple-element.5) | copy-start | bytes 49156

commit v4 on v3

--- a/solution.py
+++ b/solution.py
@@ -12,8 +12,10 @@
 lam_low = 0.05
 lam_high = 2.0
 LANES = 128
-VMEM_LIMIT = 62 * 1024 * 1024
+VMEM_LIMIT = 65600000
 GROUP = 512
+HOST_GROUP = 512
+HOME_GROUP = 512
 PIECE = 128
 LAG = 4
 LEAD = 2
@@ -107,7 +109,8 @@
         remote(src(to), dst.at[me], send_sem.at[off], recv_sem.at[off], target(to)).start()
         return 0
 
-    lax.fori_loop(1, peers, start, 0)
+    lax.fori_loop(0, peers // 2, lambda i, _: start(2 * i + 1, _), 0)
+    lax.fori_loop(1, peers // 2, lambda i, _: start(2 * i, _), 0)
 
 
 def exchange_wait(place, src, dst, send_sem, recv_sem):
@@ -138,10 +141,12 @@
     num_edges = wide_rows * LANES
     num_rows = out_ref.shape[0]
     high = num_rows // LANES
-    ktile = min(1024, num_edges)
+    ktile = min(2048, num_edges)
     etile = 1024
     quarter = num_edges // 4
     groups = num_rows // GROUP
+    host_groups, home_groups = num_rows // HOST_GROUP, num_rows // HOME_GROUP
+    host_pairs = HOST_GROUP // PIECE // 2
     per = GROUP // PIECE
     count = num_rows // PIECE
     core, half = lax.rem(me, 2), z // 2
@@ -370,17 +375,17 @@
             src.at[s, rows], dst.at[s, rows], line_sem.at[0, s, kind, k], line_sem.at[1, s, land, k], target
         )
 
-    def own_rows(s, c, place, edges):
-        at = pl.multiple_of(c * GROUP, GROUP)
-        local = scatter_rows(at, GROUP, edges)
+    def own_rows(s, c, place, edges, size):
+        at = pl.multiple_of(c * size, size)
+        local = scatter_rows(at, size, edges)
 
         @pl.when(c == 0)
         def _():
             exchange_wait(*back_of(s, place))
             retb[...] = pair(back[s].reshape(halo_len, columns))
 
-        pick = one_hot(down_rows(listrow[min(edges, 1) : min(edges, 1) + 1, :], at, GROUP))
-        own[s, pl.ds(at, GROUP), :] = local + halves(dot(pick, retb[...]))
+        pick = one_hot(down_rows(listrow[min(edges, 1) : min(edges, 1) + 1, :], at, size))
+        own[s, pl.ds(at, size), :] = local + halves(dot(pick, retb[...]))
 
     def update(s, rows, keep, push, last):
         old = dirn[rows, :]
@@ -419,12 +424,12 @@
         sends = jnp.logical_or(u == 0, u == 3)
 
         def group_rows(c, _):
-            own_rows(0, c, at_home, 0)
+            own_rows(0, c, at_home, 0, HOME_GROUP)
 
             @pl.when(sends)
             def _():
-                for j in range(per):
-                    to_inward(c * per + j).start()
+                for j in range(HOME_GROUP // PIECE):
+                    to_inward(c * (HOME_GROUP // PIECE) + j).start()
 
             @pl.when(c == 0)
             def _():
@@ -435,6 +440,8 @@
                 def _():
                     degree_sum().start()
 
+            @pl.when(c == 1)
+            def _():
                 @pl.when(moves)
                 def _():
                     for copy in swaps():
@@ -442,7 +449,7 @@
 
                 spread_columns()
 
-            @pl.when(jnp.logical_and(u == 2, c == groups - 2))
+            @pl.when(jnp.logical_and(u == 2, c == home_groups - 2))
             def _():
                 degree_sum().wait_recv()
                 degmine[...] = degown[...] + degouter[...]
@@ -452,7 +459,7 @@
 
             return 0
 
-        lax.fori_loop(0, groups, group_rows, 0)
+        lax.fori_loop(0, home_groups, group_rows, 0)
 
         @pl.when(u == 1)
         def _():
@@ -499,7 +506,7 @@
             def _():
                 pick_group(0, group)
 
-            @pl.when(group > 0)
+            @pl.when(jnp.logical_and(group > 0, k < count - per // 2))
             def _():
                 gather_near(group - 1, j)
 
@@ -563,17 +570,17 @@
             return line_copy(s, 2, 2, k, total, total, other_core)
 
         def pair_sum(c):
-            for j in range(per // 2):
-                k = c * per + 2 * j + core
+            for j in range(host_pairs):
+                k = (c * host_pairs + j) * 2 + core
                 rows = piece_rows(k)
                 lend(k).wait_recv()
                 mine[s, rows, :] = own[s, rows, :] + outer[s, rows, :]
                 cross(k).start()
 
         def group_rows(c, _):
-            own_rows(s, c, at_host, 4)
-            for j in range(per // 2):
-                lend(c * per + 2 * j + 1 - core).start()
+            own_rows(s, c, at_host, 4, HOST_GROUP)
+            for j in range(host_pairs):
+                lend((c * host_pairs + j) * 2 + 1 - core).start()
 
             @pl.when(c > 0)
             def _():
@@ -581,8 +588,8 @@
 
             return 0
 
-        lax.fori_loop(0, groups, group_rows, 0)
-        pair_sum(groups - 1)
+        lax.fori_loop(0, host_groups, group_rows, 0)
+        pair_sum(host_groups - 1)
 
         def step(m, _):
             k = 2 * m + core
@@ -590,6 +597,13 @@
             cross(k).wait_recv()
             total[s, rows, :] = mine[s, rows, :] + inner[s, rows, :]
             share(k).start()
+            group, j = m // (per // 2), lax.rem(m, per // 2)
+
+            @pl.when(jnp.logical_and(group > 0, m < count // 2 - 1))
+            def _():
+                gather_near(group - 1, 2 * j)
+                gather_near(group - 1, 2 * j + 1)
+
             share(2 * m + 1 - core).wait_recv()
             update(s, pl.ds(pl.multiple_of(m * 2 * PIECE, 2 * PIECE), 2 * PIECE), keep, push, last)
 
@@ -601,16 +615,9 @@
             def _():
                 forward(m - LEAD)
 
-            group, j = m // (per // 2), lax.rem(m, per // 2)
-
             @pl.when(j == per // 2 - 1)
             def _():
                 pick_group(s, group)
-
-            @pl.when(group > 0)
-            def _():
-                gather_near(group - 1, 2 * j)
-                gather_near(group - 1, 2 * j + 1)
 
             return 0
 
@@ -645,6 +652,12 @@
         land_args = (at_host, listed_of, landed.at[s], land_sem.at[0, s], land_sem.at[1, s])
         exchange(*land_args)
         landed[s, block] = listed[s, pl.ds(pl.multiple_of(block * slot, 8), slot), :]
+
+        def near_left(q, _):
+            gather_near(groups - 2, q)
+            return 0
+
+        lax.fori_loop(per // 2, per, near_left, 0)
 
         def near_tail(q, _):
             gather_near(groups - 1, q, True)
@@ -747,7 +760,7 @@
         vmem((halo_len, LANES), i32), vmem((2, halo_len), i32),
         rows_f32, rows_f32, rows_f32, rows_f32, rows_f32,
         vmem((num_rows + halo_len, 2 * columns), bf16), vmem((num_edges, columns), f32),
-        vmem((GROUP, 2 * columns), f32), vmem((halo_len, 2 * columns), bf16),
+        vmem((max(512, GROUP, HOST_GROUP, HOME_GROUP), 2 * columns), f32), vmem((halo_len, 2 * columns), bf16),
         vmem((num_edges, 2 * columns), bf16), line, line, line, line, line,
         flat_halo, halo, flat_halo, halo,
         vmem((wide_rows, LANES), f32), vmem((peers8, LANES), i32),
@@ -763,7 +776,7 @@
         functools.partial(kernel, peers),
         in_specs=[in_vmem] * 6 + [pl.BlockSpec(memory_space=pltpu.SMEM)],
         out_specs=[in_vmem] * 2,
-        out_shape=[jax.ShapeDtypeStruct((num_rows, columns), f32), jax.ShapeDtypeStruct((wide_rows, LANES), f32)],
+        out_shape=[pltpu.VMEM((num_rows, columns), f32), pltpu.VMEM((wide_rows, LANES), f32)],
         scratch_shapes=scratch,
         compiler_params=pltpu.CompilerParams(collective_id=0, has_side_effects=True, vmem_limit_bytes=VMEM_LIMIT),
         name="sketch",

time: 139 us -> 128 us (0.921)
  Pallas kernels: 134 us -> 125 us
    pallas_call x1, Pallas kernels: 134 us -> 125 us  [local(): pl.pallas_call(functools.partial(kernel, peers), in_specs=[in_vmem] * 6 +...]
    unnamed x4 -> x2, local copies, waits for them, and re-layouts: 2.88 us -> 1.58 us
where the time goes in v4:
time: 128 us
  Pallas kernels  125 us (98%)
  local copies, waits for them, and re-layouts  1.58 us (1%)
  between operations  1.29 us (1%)
    pallas_call x1, Pallas kernels, local(): pl.pallas_call(functools.partial(kernel, peers), in_specs=[in_vmem] * 6 +...  125 us

profile of v4, /device:TPU:9, one launch (start us, length us, event | category | flops | bytes accessed | tf_op | source)
XLA Modules:
  0.0 127.9 jit_solution(16247824642869349226)
XLA Ops:
  1.3 125.0 %sketch.1 = (f32[2048,128]{1,0:T(8,128)S(1)}, f32[32,128]{1,0:T(8,128)S(1)}) custom-call(bf16[4096,128]{1,0:T(8,128)(2,1)} %sketch_ref.1, f32[32,128]{1,0:T(8,128)} %bitcast.7, f32[16,128]{1,0:T(8,128)} %bitcast.10, s32[32,128]{1,0:T(8,128)} %bitcast.8, s32[32,128]{1,0:T(8,128)} %bitcast.9, s32[8,48]{1,0:T(8,128)} %bitcast.11, s32[1]{0:T(128)S(6)} %copy.13.count_ref), custom_call_target="tpu_custom_call" | custom-call | tf_op jit(solution)/shard_map/sketch/pallas_call | solution.py:775
  126.3 1.0 copy.11
  127.3 0.6 copy.12

commit v5 on v4

--- a/solution.py
+++ b/solution.py
@@ -17,7 +17,8 @@
 HOST_GROUP = 512
 HOME_GROUP = 512
 PIECE = 128
-LAG = 4
+LAG = 8
+HOLD = 1
 LEAD = 2
 
 
@@ -423,13 +424,20 @@
 
         sends = jnp.logical_or(u == 0, u == 3)
 
+        def send_group(c):
+            for j in range(HOME_GROUP // PIECE):
+                to_inward(c * (HOME_GROUP // PIECE) + j).start()
+
         def group_rows(c, _):
             own_rows(0, c, at_home, 0, HOME_GROUP)
 
-            @pl.when(sends)
-            def _():
-                for j in range(HOME_GROUP // PIECE):
-                    to_inward(c * (HOME_GROUP // PIECE) + j).start()
+            @pl.when(u == 3)
+            def _():
+                send_group(c)
+
+            @pl.when(jnp.logical_and(u == 0, c >= HOLD))
+            def _():
+                send_group(c - HOLD)
 
             @pl.when(c == 0)
             def _():
@@ -440,7 +448,15 @@
                 def _():
                     degree_sum().start()
 
-            @pl.when(c == 1)
+            @pl.when(jnp.logical_and(u == 2, c == home_groups - 2))
+            def _():
+                degree_sum().wait_recv()
+                degmine[...] = degown[...] + degouter[...]
+                degree_part().start()
+                for k in range(LAG // 2):
+                    pass_partial(k)
+
+            @pl.when(c == home_groups - 2)
             def _():
                 @pl.when(moves)
                 def _():
@@ -449,17 +465,19 @@
 
                 spread_columns()
 
-            @pl.when(jnp.logical_and(u == 2, c == home_groups - 2))
-            def _():
-                degree_sum().wait_recv()
-                degmine[...] = degown[...] + degouter[...]
-                degree_part().start()
-                for k in range(LAG):
+            @pl.when(jnp.logical_and(u == 2, c == home_groups - 1))
+            def _():
+                for k in range(LAG // 2, LAG):
                     pass_partial(k)
 
             return 0
 
         lax.fori_loop(0, home_groups, group_rows, 0)
+
+        @pl.when(u == 0)
+        def _():
+            for c in range(home_groups - HOLD, home_groups):
+                send_group(c)
 
         @pl.when(u == 1)
         def _():

time: 128 us -> 125 us (0.977)
  Pallas kernels: 125 us -> 122 us
    pallas_call x1, Pallas kernels: 125 us -> 122 us  [local(): pl.pallas_call(functools.partial(kernel, peers), in_specs=[in_vmem] * 6 +...]
where the time goes in v5:
time: 125 us
  Pallas kernels  122 us (98%)
  local copies, waits for them, and re-layouts  1.58 us (1%)
  between operations  1.29 us (1%)
    pallas_call x1, Pallas kernels, local(): pl.pallas_call(functools.partial(kernel, peers), in_specs=[in_vmem] * 6 +...  122 us

profile of v5, /device:TPU:9, one launch (start us, length us, event | category | flops | bytes accessed | tf_op | source)
XLA Modules:
  0.0 125.2 jit_solution(4380701822246505302)
XLA Ops:
  1.3 122.3 %sketch.1 = (f32[2048,128]{1,0:T(8,128)S(1)}, f32[32,128]{1,0:T(8,128)S(1)}) custom-call(bf16[4096,128]{1,0:T(8,128)(2,1)} %sketch_ref.1, f32[32,128]{1,0:T(8,128)} %bitcast.7, f32[16,128]{1,0:T(8,128)} %bitcast.10, s32[32,128]{1,0:T(8,128)} %bitcast.8, s32[32,128]{1,0:T(8,128)} %bitcast.9, s32[8,48]{1,0:T(8,128)} %bitcast.11, s32[1]{0:T(128)S(6)} %copy.13.count_ref), custom_call_target="tpu_custom_call" | custom-call | tf_op jit(solution)/shard_map/sketch/pallas_call | solution.py:793
  123.6 1.0 copy.11
  124.6 0.6 copy.12
